TPU v7x, 256 devices: a whole 4x4x8 slice. The times are simulated.
256 devices in a mesh: row: 16 (over z_lo, x), col: 16 (over y, z_hi, core).
Axes of the slice: x: 4, y: 4, z: 8 (z_hi: 2, z_lo: 4; z = z_hi * 4 + z_lo), core: 2. Of those that a mesh axis runs over, the one named last changes fastest.
Arguments:
- inverse_block: bfloat16 [10240, 10240], P('row', 'col'), may hold values from -6 to 6
- factor_cols: bfloat16 [10240, 4096], P('row', 'col'), may hold values from -0.078125 to 0.078125
- diag_inverse: float32 [16, 256, 256], P('col', 'row'), may hold values from -6 to 6
- fill_mask: int32 [40, 16], replicated, may hold values from 0 to 1
Outputs:
- inverse_cols: bfloat16 [10240, 4096], P('row', 'col')
- inverse_diag: float32 [16, 256, 256], P('col', 'row')
All inputs are finite; a program needn't handle non-finite values.
Results may differ from a plain program's by a relative error of at most 0.0027.
Values may be sent and summed in bfloat16 or wider, within the bound.
No kernel may reach another device: no remote copies, remote signals or barrier semaphores. Data moves between devices by JAX's collectives and lax.ppermute only.
A program may use at most 64 MiB of HBM per device.

v0:
```python
import jax
import jax.numpy as jnp
from jax import lax
from jax.sharding import Mesh, PartitionSpec as P


AXES = ("zl", "x", "y", "zh", "core")
SIZES = (4, 4, 4, 2, 2)


def _places():
    for zl in range(4):
        for x in range(4):
            for y in range(4):
                for zh in range(2):
                    for core in range(2):
                        yield zl, x, y, zh, core


def _index(place):
    out = 0
    for value, size in zip(place, SIZES):
        out = out * size + value % size
    return out


def _move(value, target, senders=None):
    pairs = [
        (_index(p), _index(target(*p)))
        for p in _places()
        if senders is None or senders(*p)
    ]
    return lax.ppermute(value, AXES, pairs)


def _matched(zl, x, y, zh, core):
    return x % 2 == core


def body(inverse_block, factor_cols, diag_inverse, fill_mask):
    rows, cols = factor_cols.shape
    zl, x, y, zh, core = (lax.axis_index(a) for a in AXES)
    row = zl * 4 + x
    col = y * 4 + zh * 2 + core

    halves = jnp.repeat(fill_mask, 2, axis=0)
    pieces = rows // 128
    mask = lax.dynamic_slice(halves, (row * pieces, col), (pieces, 1)).reshape(pieces, 1, 1)

    own = inverse_block
    far = _move(own, lambda zl, x, y, zh, c: (zl, x, y, zh + 1, c))

    def along_y(v):
        return jnp.stack([
            v,
            _move(v, lambda zl, x, y, zh, c: (zl, x, y - 1, zh, c)),
            _move(v, lambda zl, x, y, zh, c: (zl, x, y + 2, zh, c)),
            _move(v, lambda zl, x, y, zh, c: (zl, x, y + 1, zh, c)),
        ])

    near_blocks = along_y(own)
    far_blocks = along_y(far)

    selected = (factor_cols.reshape(pieces, 128, cols) * mask.astype(jnp.bfloat16)).reshape(rows, cols)
    other = _move(selected, lambda zl, x, y, zh, c: (zl, x, y, zh, 1 - c),
                  lambda zl, x, y, zh, c: x % 2 != c)
    line = [jnp.concatenate([selected, other], axis=1)]
    for d in (1, 2, 3):
        line.append(_move(line[0], lambda zl, x, y, zh, c: (zl - d, x, y, zh, c), _matched))

    is_matched = (x % 2) == core
    first_near = (jnp.where(is_matched, x, (x + 3) % 4) // 2) == zh
    total = None
    for d, v in enumerate(line):
        right = _move(v, lambda zl, x, y, zh, c: (zl, x + 1, y, zh, c), _matched)
        left = _move(v, lambda zl, x, y, zh, c: (zl, x - 1, y, zh, c), _matched)
        across = _move(v, lambda zl, x, y, zh, c: (zl, x + 2, y, zh, c), _matched)
        if total is not None:
            total, right, left, across = lax.optimization_barrier((total, right, left, across))
        first = jnp.where(is_matched, v, right)
        second = jnp.where(is_matched, across, left)
        place = (zl + d - y) % 4
        for blocks, piece in (
            (near_blocks, jnp.where(first_near, first, second)),
            (far_blocks, jnp.where(first_near, second, first)),
        ):
            block = lax.dynamic_index_in_dim(blocks, place, 0, keepdims=False)
            product = jnp.dot(block, piece, preferred_element_type=jnp.float32)
            total = product if total is None else total + product

    theirs = _move(total[:, cols:], lambda zl, x, y, zh, c: (zl, x, y, zh, 1 - c))
    summed = (total[:, :cols] + theirs).reshape(pieces, 128, cols)
    inverse_cols = (-summed * mask.astype(jnp.float32)).astype(jnp.bfloat16).reshape(rows, cols)

    part = jnp.einsum("ia,ib->ab", selected, inverse_cols, preferred_element_type=jnp.float32)
    shares = lax.all_to_all(part.reshape(16, cols // 16, cols), ("zl", "x"), 0, 0)
    inverse_diag = diag_inverse - jnp.sum(shares, axis=0)[None]
    return inverse_cols, inverse_diag


def solution(mesh):
    fine = Mesh(mesh.devices.reshape(SIZES), AXES)
    row, col = ("zl", "x"), ("y", "zh", "core")
    return jax.shard_map(
        body,
        mesh=fine,
        in_specs=(P(row, col), P(row, col), P(col, row, None), P()),
        out_specs=(P(row, col), P(col, row, None)),
        check_vma=False,
    )
```

profile of v0, /device:TPU:8, one launch (start us, length us, event | category | flops | bytes accessed | tf_op | source)
XLA Modules:
  0.0 156.5 jit_solution(5833472498637576237)
XLA Ops:
  0.6 7.3 %collective-permute-start.7 = (bf16[640,640]{1,0:T(8,128)(2,1)}, bf16[640,640]{1,0:T(8,128)(2,1)S(1)}, u32[]{:S(2)}, u32[]{:S(2)}) collective-permute-start(bf16[640,640]{1,0:T(8,128)(2,1)} %param.4), channel_id=1, source_target_pairs={{0,2},{1,3},{2,0},{3,1},{4,6},{5,7},{6,4},{7,5},{8,10},{9,11},{10,... | collective-permute-start | bytes 2457608 | tf_op jit(solution)/shard_map/ppermute | solution.py:33
  7.9 0.8 copy.9
  9.0 1.2 copy.10
  10.2 1.3 collective-permute-start.3
  12.0 2.6 %collective-permute-start.1 = (bf16[640,640]{1,0:T(8,128)(2,1)S(1)}, bf16[640,640]{1,0:T(8,128)(2,1)S(1)}, u32[]{:S(2)}, u32[]{:S(2)}) collective-permute-start(bf16[640,640]{1,0:T(8,128)(2,1)S(1)} %copy-done.1), channel_id=1, source_target_pairs={{0,8},{1,9},{2,10},{3,11},{4,12},{5,13},{6,14},{7,15},{8,0},{9,1},... | collective-permute-start | bytes 2457608 | tf_op jit(solution)/shard_map/ppermute | solution.py:33
  14.6 1.9 %collective-permute-start.2 = (bf16[640,640]{1,0:T(8,128)(2,1)S(1)}, bf16[640,640]{1,0:T(8,128)(2,1)S(1)}, u32[]{:S(2)}, u32[]{:S(2)}) collective-permute-start(bf16[640,640]{1,0:T(8,128)(2,1)S(1)} %copy-done.1), channel_id=1, source_target_pairs={{0,4},{1,5},{2,6},{3,7},{4,8},{5,9},{6,10},{7,11},{8,12},{9,13},{1... | collective-permute-start | bytes 2457608 | tf_op jit(solution)/shard_map/ppermute | solution.py:33
  16.5 0.9 pad_maximum_fusion.2
  17.4 3.6 %collective-permute-start.4 = (bf16[640,512]{0,1:T(8,128)(2,1)}, bf16[640,512]{0,1:T(8,128)(2,1)S(1)}, u32[]{:S(2)}, u32[]{:S(2)}) collective-permute-start(bf16[640,512]{0,1:T(8,128)(2,1)} %pad_maximum_fusion.2), channel_id=1, source_target_pairs={{0,16},{2,18},{4,20},{6,22},{8,24},{10,26},{12,28},{14,30},{17,33}... | collective-permute-start | bytes 1966088 | tf_op jit(solution)/shard_map/ppermute | solution.py:33
  21.0 21.7 %collective-permute-done.7 = bf16[640,640]{1,0:T(8,128)(2,1)S(1)} collective-permute-done((bf16[640,640]{1,0:T(8,128)(2,1)}, bf16[640,640]{1,0:T(8,128)(2,1)S(1)}, u32[]{:S(2)}, u32[]{:S(2)}) %collective-permute-start.7) | collective-permute-done | bytes 819232 | tf_op jit(solution)/shard_map/ppermute | solution.py:33
  42.7 4.9 %collective-permute-start.5 = (bf16[640,512]{0,1:T(8,128)(2,1)}, bf16[640,512]{0,1:T(8,128)(2,1)S(1)}, u32[]{:S(2)}, u32[]{:S(2)}) collective-permute-start(bf16[640,512]{0,1:T(8,128)(2,1)} %pad_maximum_fusion.2), channel_id=1, source_target_pairs={{0,32},{2,34},{4,36},{6,38},{8,40},{10,42},{12,44},{14,46},{17,49}... | collective-permute-start | bytes 1966088 | tf_op jit(solution)/shard_map/ppermute | solution.py:33
  47.6 2.2 %collective-permute-start.6 = (bf16[640,512]{0,1:T(8,128)(2,1)}, bf16[640,512]{0,1:T(8,128)(2,1)}, u32[]{:S(2)}, u32[]{:S(2)}) collective-permute-start(bf16[640,512]{0,1:T(8,128)(2,1)} %pad_maximum_fusion.2), channel_id=1, source_target_pairs={{0,48},{2,50},{4,52},{6,54},{8,56},{10,58},{12,60},{14,62},{17,1},... | collective-permute-start | bytes 1966088 | tf_op jit(solution)/shard_map/ppermute | solution.py:33
  49.8 1.3 collective-permute-done.1
  51.4 0.9 collective-permute-done.2
  52.3 3.2 %collective-permute-start.8 = (bf16[640,640]{1,0:T(8,128)(2,1)S(1)}, bf16[640,640]{1,0:T(8,128)(2,1)}, u32[]{:S(2)}, u32[]{:S(2)}) collective-permute-start(bf16[640,640]{1,0:T(8,128)(2,1)S(1)} %collective-permute-done.7), channel_id=1, source_target_pairs={{0,12},{1,13},{2,14},{3,15},{4,0},{5,1},{6,2},{7,3},{8,4},{9,5},{1... | collective-permute-start | bytes 2457608 | tf_op jit(solution)/shard_map/ppermute | solution.py:33
  55.5 4.5 %collective-permute-start.9 = (bf16[640,640]{1,0:T(8,128)(2,1)S(1)}, bf16[640,640]{1,0:T(8,128)(2,1)}, u32[]{:S(2)}, u32[]{:S(2)}) collective-permute-start(bf16[640,640]{1,0:T(8,128)(2,1)S(1)} %collective-permute-done.7), channel_id=1, source_target_pairs={{0,8},{1,9},{2,10},{3,11},{4,12},{5,13},{6,14},{7,15},{8,0},{9,1},... | collective-permute-start | bytes 2457608 | tf_op jit(solution)/shard_map/ppermute | solution.py:33
  60.0 0.9 copy-done.6
  60.9 3.8 %collective-permute-start.11 = (bf16[640,512]{0,1:T(8,128)(2,1)}, bf16[640,512]{0,1:T(8,128)(2,1)}, u32[]{:S(2)}, u32[]{:S(2)}) collective-permute-start(bf16[640,512]{0,1:T(8,128)(2,1)} %pad_maximum_fusion.2), channel_id=1, source_target_pairs={{0,192},{2,194},{4,196},{6,198},{8,200},{10,202},{12,204},{14,206}... | collective-permute-start | bytes 1966088 | tf_op jit(solution)/shard_map/ppermute | solution.py:33
  64.7 2.5 %collective-permute-start.15 = (bf16[640,512]{0,1:T(8,128)(2,1)}, bf16[640,512]{0,1:T(8,128)(2,1)}, u32[]{:S(2)}, u32[]{:S(2)}) collective-permute-start(bf16[640,512]{0,1:T(8,128)(2,1)} %pad_maximum_fusion.2), channel_id=1, source_target_pairs={{0,128},{2,130},{4,132},{6,134},{8,136},{10,138},{12,140},{14,142}... | collective-permute-start | bytes 1966088 | tf_op jit(solution)/shard_map/ppermute | solution.py:33
  67.3 1.7 %pad_maximum_fusion = bf16[4,640,640]{2,1,0:T(8,128)(2,1)S(1)} fusion(bf16[1,640,640]{2,1,0:T(8,128)(2,1)} %bitcast.57, bf16[1,640,640]{2,1,0:T(8,128)(2,1)} %bitcast.56, bf16[1,640,640]{2,1,0:T(8,128)(2,1)S(1)} %bitcast.55, bf16[1,640,640]{2,1,0:T(8,128)(2,1)S(1)} %bitcast.53), kind=kLoop, calls=%fused_computation | loop fusion | flops 4915200 | bytes 6553600 | tf_op jit(solution)/shard_map/stack | solution.py:54
  69.0 4.7 %collective-permute-done.11 = bf16[640,512]{0,1:T(8,128)(2,1)} collective-permute-done((bf16[640,512]{0,1:T(8,128)(2,1)}, bf16[640,512]{0,1:T(8,128)(2,1)}, u32[]{:S(2)}, u32[]{:S(2)}) %collective-permute-start.11) | collective-permute-done | bytes 655392 | tf_op jit(solution)/shard_map/ppermute | solution.py:33
  73.7 2.9 %collective-permute-start.19 = (bf16[640,512]{0,1:T(8,128)(2,1)}, bf16[640,512]{0,1:T(8,128)(2,1)S(1)}, u32[]{:S(2)}, u32[]{:S(2)}) collective-permute-start(bf16[640,512]{0,1:T(8,128)(2,1)} %pad_maximum_fusion.2), channel_id=1, source_target_pairs={{0,64},{2,66},{4,68},{6,70},{8,72},{10,74},{12,76},{14,78},{17,81}... | collective-permute-start | bytes 1966088 | tf_op jit(solution)/shard_map/ppermute | solution.py:33
  76.6 1.3 collective-permute-start.12
  78.0 1.3 collective-permute-start.13
  79.3 13.5 %collective-permute-done.9 = bf16[640,640]{1,0:T(8,128)(2,1)} collective-permute-done((bf16[640,640]{1,0:T(8,128)(2,1)S(1)}, bf16[640,640]{1,0:T(8,128)(2,1)}, u32[]{:S(2)}, u32[]{:S(2)}) %collective-permute-start.9) | collective-permute-done | bytes 819232 | tf_op jit(solution)/shard_map/ppermute | solution.py:33
  92.8 4.8 %collective-permute-start.14 = (bf16[640,512]{0,1:T(8,128)(2,1)}, bf16[640,512]{0,1:T(8,128)(2,1)S(1)}, u32[]{:S(2)}, u32[]{:S(2)}) collective-permute-start(bf16[640,512]{0,1:T(8,128)(2,1)} %collective-permute-done.11), channel_id=1, source_target_pairs={{0,32},{2,34},{4,36},{6,38},{8,40},{10,42},{12,44},{14,46},{17,49}... | collective-permute-start | bytes 1966088 | tf_op jit(solution)/shard_map/ppermute | solution.py:33
  97.6 2.0 %pad_maximum_fusion.1 = bf16[4,640,640]{2,1,0:T(8,128)(2,1)S(1)} fusion(bf16[1,640,640]{2,1,0:T(8,128)(2,1)} %bitcast.10, bf16[1,640,640]{2,1,0:T(8,128)(2,1)} %bitcast.9, bf16[1,640,640]{2,1,0:T(8,128)(2,1)} %bitcast.8, bf16[1,640,640]{2,1,0:T(8,128)(2,1)S(1)} %bitcast.54), kind=kLoop, calls=%fused_computation.1 | loop fusion | flops 4915200 | bytes 6553600 | tf_op jit(solution)/shard_map/stack | solution.py:54
  99.6 1.3 collective-permute-start.16
  101.0 0.8 fusion.12
  101.8 0.8 convolution_add_fusion
  102.6 1.3 collective-permute-start.17
  103.9 2.6 %collective-permute-start.18 = (bf16[640,512]{0,1:T(8,128)(2,1)}, bf16[640,512]{0,1:T(8,128)(2,1)S(1)}, u32[]{:S(2)}, u32[]{:S(2)}) collective-permute-start(bf16[640,512]{0,1:T(8,128)(2,1)} %collective-permute-done.15), channel_id=1, source_target_pairs={{0,32},{2,34},{4,36},{6,38},{8,40},{10,42},{12,44},{14,46},{17,49}... | collective-permute-start | bytes 1966088 | tf_op jit(solution)/shard_map/ppermute | solution.py:33
  106.5 1.3 collective-permute-start.20
  107.9 1.3 collective-permute-start.21
  109.2 1.9 %fusion.10 = f32[640,512]{1,0:T(8,128)S(1)} fusion(bf16[4,640,640]{2,1,0:T(8,128)(2,1)S(1)} %pad_maximum_fusion, s32[]{:T(128)S(6)} %select_n.142, pred[]{:T(512)S(6)} %eq.14, bf16[640,512]{0,1:T(8,128)(2,1)} %collective-permute-done.11, bf16[640,512]{0,1:T(8,128)(2,1)S(1)} %collective-permute-done.12, pred[]{:T(512)S(6)} %eq.13, ...), kind=kOutput, calls=%fused_computation.16 | convolution fusion | flops 420413440 | bytes 4751366 | tf_op jit(solution)/shard_map/dot_general | solution.py:88
  111.1 1.9 %add_add_fusion.2 = f32[640,512]{1,0:T(8,128)S(1)} fusion(f32[640,512]{1,0:T(8,128)S(1)} %convolution_add_fusion, f32[640,512]{1,0:T(8,128)S(1)} %fusion.10, bf16[4,640,640]{2,1,0:T(8,128)(2,1)S(1)} %pad_maximum_fusion.1, s32[]{:T(128)S(6)} %select_n.142, pred[]{:T(512)S(6)} %eq.14, bf16[640,512]{0,1:T(8,128)(2,1)} %collective-permute-done.11, ...), kind=kOutput, calls=%fused_computation.5 | convolution fusion | flops 421068800 | bytes 7372806 | tf_op jit(solution)/shard_map/dot_general | solution.py:88
  113.0 4.9 %collective-permute-start.22 = (bf16[640,512]{0,1:T(8,128)(2,1)S(1)}, bf16[640,512]{0,1:T(8,128)(2,1)S(1)}, u32[]{:S(2)}, u32[]{:S(2)}) collective-permute-start(bf16[640,512]{0,1:T(8,128)(2,1)S(1)} %collective-permute-done.19), channel_id=1, source_target_pairs={{0,32},{2,34},{4,36},{6,38},{8,40},{10,42},{12,44},{14,46},{17,49}... | collective-permute-start | bytes 1966088 | tf_op jit(solution)/shard_map/ppermute | solution.py:33
  117.9 1.4 collective-permute-done.17
  119.3 1.8 %collective-permute-done.18 = bf16[640,512]{0,1:T(8,128)(2,1)S(1)} collective-permute-done((bf16[640,512]{0,1:T(8,128)(2,1)}, bf16[640,512]{0,1:T(8,128)(2,1)S(1)}, u32[]{:S(2)}, u32[]{:S(2)}) %collective-permute-start.18) | collective-permute-done | bytes 655392 | tf_op jit(solution)/shard_map/ppermute | solution.py:33
  121.2 1.9 %fusion.6 = f32[640,512]{1,0:T(8,128)S(1)} fusion(bf16[4,640,640]{2,1,0:T(8,128)(2,1)S(1)} %pad_maximum_fusion, s32[]{:T(128)S(6)} %select_n.148, pred[]{:T(512)S(6)} %eq.14, bf16[640,512]{0,1:T(8,128)(2,1)} %collective-permute-done.15, bf16[640,512]{0,1:T(8,128)(2,1)S(1)} %collective-permute-done.16, pred[]{:T(512)S(6)} %eq.13, ...), kind=kOutput, calls=%fused_computation.12 | convolution fusion | flops 420413440 | bytes 4751366 | tf_op jit(solution)/shard_map/dot_general | solution.py:88
  123.0 1.9 %add_add_fusion.1 = f32[640,512]{1,0:T(8,128)S(1)} fusion(f32[640,512]{1,0:T(8,128)S(1)} %add_add_fusion.2, f32[640,512]{1,0:T(8,128)S(1)} %fusion.6, bf16[4,640,640]{2,1,0:T(8,128)(2,1)S(1)} %pad_maximum_fusion.1, s32[]{:T(128)S(6)} %select_n.148, pred[]{:T(512)S(6)} %eq.14, bf16[640,512]{0,1:T(8,128)(2,1)} %collective-permute-done.15, ...), kind=kOutput, calls=%fused_computation.4 | convolution fusion | flops 421068800 | bytes 7372806 | tf_op jit(solution)/shard_map/dot_general | solution.py:88
  124.9 2.1 %collective-permute-done.20 = bf16[640,512]{0,1:T(8,128)(2,1)S(1)} collective-permute-done((bf16[640,512]{0,1:T(8,128)(2,1)S(1)}, bf16[640,512]{0,1:T(8,128)(2,1)S(1)}, u32[]{:S(2)}, u32[]{:S(2)}) %collective-permute-start.20) | collective-permute-done | bytes 655392 | tf_op jit(solution)/shard_map/ppermute | solution.py:33
  127.0 6.3 %collective-permute-done.21 = bf16[640,512]{0,1:T(8,128)(2,1)S(1)} collective-permute-done((bf16[640,512]{0,1:T(8,128)(2,1)S(1)}, bf16[640,512]{0,1:T(8,128)(2,1)S(1)}, u32[]{:S(2)}, u32[]{:S(2)}) %collective-permute-start.21) | collective-permute-done | bytes 655392 | tf_op jit(solution)/shard_map/ppermute | solution.py:33
  133.3 1.9 %collective-permute-done.22 = bf16[640,512]{0,1:T(8,128)(2,1)S(1)} collective-permute-done((bf16[640,512]{0,1:T(8,128)(2,1)S(1)}, bf16[640,512]{0,1:T(8,128)(2,1)S(1)}, u32[]{:S(2)}, u32[]{:S(2)}) %collective-permute-start.22) | collective-permute-done | bytes 655392 | tf_op jit(solution)/shard_map/ppermute | solution.py:33
  135.2 0.8 fusion.2
  135.9 0.8 add_add_fusion
  137.2 1.8 %collective-permute-done.23 = f32[640,256]{1,0:T(8,128)S(1)} collective-permute-done((f32[640,256]{1,0:T(8,128)S(1)}, f32[640,256]{1,0:T(8,128)S(1)}, u32[]{:S(2)}, u32[]{:S(2)}) %collective-permute-start.23) | collective-permute-done | bytes 655392 | tf_op jit(solution)/shard_map/ppermute | solution.py:33
  139.5 16.4 %all_to_all.5 = f32[16,16,256]{2,1,0:T(8,128)S(1)} all-to-all(f32[16,16,256]{2,1,0:T(8,128)S(1)} %fusion.48), channel_id=1, replica_groups=mesh['zl'=4,'x'=4,'y'=4,'zh'=2,'core'=2] {'zl','x'}, dimensions={0} | all-to-all | bytes 524288 | tf_op jit(solution)/shard_map/all_to_all | solution.py:96
  155.9 0.6 bitcast_subtract_fusion
  (43 shorter events, 2.2 us)
Async XLA Ops:
  0.6 10.9 %copy-start.1 = (bf16[640,640]{1,0:T(8,128)(2,1)S(1)}, bf16[640,640]{1,0:T(8,128)(2,1)}, u32[]{:S(2)}) copy-start(bf16[640,640]{1,0:T(8,128)(2,1)} %param.4) | copy-start | bytes 2457604
  0.6 42.1 %collective-permute-start.7 = (bf16[640,640]{1,0:T(8,128)(2,1)}, bf16[640,640]{1,0:T(8,128)(2,1)S(1)}, u32[]{:S(2)}, u32[]{:S(2)}) collective-permute-start(bf16[640,640]{1,0:T(8,128)(2,1)} %param.4), channel_id=1, source_target_pairs={{0,2},{1,3},{2,0},{3,1},{4,6},{5,7},{6,4},{7,5},{8,10},{9,11},{10,... | collective-permute-start | bytes 2457608 | tf_op jit(solution)/shard_map/ppermute | solution.py:33
  10.2 6.3 %collective-permute-start.3 = (bf16[640,256]{0,1:T(8,128)(2,1)S(1)}, bf16[640,256]{0,1:T(8,128)(2,1)S(1)}, u32[]{:S(2)}, u32[]{:S(2)}) collective-permute-start(bf16[640,256]{0,1:T(8,128)(2,1)S(1)} %broadcast_multiply_fusion), channel_id=1, source_target_pairs={{1,0},{3,2},{5,4},{7,6},{9,8},{11,10},{13,12},{15,14},{16,17},{18,... | collective-permute-start | bytes 983048 | tf_op jit(solution)/shard_map/ppermute | solution.py:33
  11.5 36.1 %collective-permute-start = (bf16[640,640]{1,0:T(8,128)(2,1)S(1)}, bf16[640,640]{1,0:T(8,128)(2,1)S(1)}, u32[]{:S(2)}, u32[]{:S(2)}) collective-permute-start(bf16[640,640]{1,0:T(8,128)(2,1)S(1)} %copy-done.1), channel_id=1, source_target_pairs={{0,12},{1,13},{2,14},{3,15},{4,0},{5,1},{6,2},{7,3},{8,4},{9,5},{1... | collective-permute-start | bytes 2457608 | tf_op jit(solution)/shard_map/ppermute | solution.py:33
  12.0 39.1 %collective-permute-start.1 = (bf16[640,640]{1,0:T(8,128)(2,1)S(1)}, bf16[640,640]{1,0:T(8,128)(2,1)S(1)}, u32[]{:S(2)}, u32[]{:S(2)}) collective-permute-start(bf16[640,640]{1,0:T(8,128)(2,1)S(1)} %copy-done.1), channel_id=1, source_target_pairs={{0,8},{1,9},{2,10},{3,11},{4,12},{5,13},{6,14},{7,15},{8,0},{9,1},... | collective-permute-start | bytes 2457608 | tf_op jit(solution)/shard_map/ppermute | solution.py:33
  14.6 37.6 %collective-permute-start.2 = (bf16[640,640]{1,0:T(8,128)(2,1)S(1)}, bf16[640,640]{1,0:T(8,128)(2,1)S(1)}, u32[]{:S(2)}, u32[]{:S(2)}) collective-permute-start(bf16[640,640]{1,0:T(8,128)(2,1)S(1)} %copy-done.1), channel_id=1, source_target_pairs={{0,4},{1,5},{2,6},{3,7},{4,8},{5,9},{6,10},{7,11},{8,12},{9,13},{1... | collective-permute-start | bytes 2457608 | tf_op jit(solution)/shard_map/ppermute | solution.py:33
  17.4 38.1 %collective-permute-start.4 = (bf16[640,512]{0,1:T(8,128)(2,1)}, bf16[640,512]{0,1:T(8,128)(2,1)S(1)}, u32[]{:S(2)}, u32[]{:S(2)}) collective-permute-start(bf16[640,512]{0,1:T(8,128)(2,1)} %pad_maximum_fusion.2), channel_id=1, source_target_pairs={{0,16},{2,18},{4,20},{6,22},{8,24},{10,26},{12,28},{14,30},{17,33}... | collective-permute-start | bytes 1966088 | tf_op jit(solution)/shard_map/ppermute | solution.py:33
  42.7 17.3 %collective-permute-start.5 = (bf16[640,512]{0,1:T(8,128)(2,1)}, bf16[640,512]{0,1:T(8,128)(2,1)S(1)}, u32[]{:S(2)}, u32[]{:S(2)}) collective-permute-start(bf16[640,512]{0,1:T(8,128)(2,1)} %pad_maximum_fusion.2), channel_id=1, source_target_pairs={{0,32},{2,34},{4,36},{6,38},{8,40},{10,42},{12,44},{14,46},{17,49}... | collective-permute-start | bytes 1966088 | tf_op jit(solution)/shard_map/ppermute | solution.py:33
  47.6 17.1 %collective-permute-start.6 = (bf16[640,512]{0,1:T(8,128)(2,1)}, bf16[640,512]{0,1:T(8,128)(2,1)}, u32[]{:S(2)}, u32[]{:S(2)}) collective-permute-start(bf16[640,512]{0,1:T(8,128)(2,1)} %pad_maximum_fusion.2), channel_id=1, source_target_pairs={{0,48},{2,50},{4,52},{6,54},{8,56},{10,58},{12,60},{14,62},{17,1},... | collective-permute-start | bytes 1966088 | tf_op jit(solution)/shard_map/ppermute | solution.py:33
  51.1 4.4 %copy-start.2 = (bf16[640,640]{1,0:T(8,128)(2,1)}, bf16[640,640]{1,0:T(8,128)(2,1)S(1)}, u32[]{:S(2)}) copy-start(bf16[640,640]{1,0:T(8,128)(2,1)S(1)} %collective-permute-done.1) | copy-start | bytes 2457604
  51.1 25.5 %collective-permute-start.10 = (bf16[640,640]{1,0:T(8,128)(2,1)S(1)}, bf16[640,640]{1,0:T(8,128)(2,1)}, u32[]{:S(2)}, u32[]{:S(2)}) collective-permute-start(bf16[640,640]{1,0:T(8,128)(2,1)S(1)} %collective-permute-done.7), channel_id=1, source_target_pairs={{0,4},{1,5},{2,6},{3,7},{4,8},{5,9},{6,10},{7,11},{8,12},{9,13},{1... | collective-permute-start | bytes 2457608 | tf_op jit(solution)/shard_map/ppermute | solution.py:33
  52.3 3.2 %copy-start.3 = (bf16[640,640]{1,0:T(8,128)(2,1)}, bf16[640,640]{1,0:T(8,128)(2,1)S(1)}, u32[]{:S(2)}) copy-start(bf16[640,640]{1,0:T(8,128)(2,1)S(1)} %collective-permute-done.2) | copy-start | bytes 2457604
  52.3 25.7 %collective-permute-start.8 = (bf16[640,640]{1,0:T(8,128)(2,1)S(1)}, bf16[640,640]{1,0:T(8,128)(2,1)}, u32[]{:S(2)}, u32[]{:S(2)}) collective-permute-start(bf16[640,640]{1,0:T(8,128)(2,1)S(1)} %collective-permute-done.7), channel_id=1, source_target_pairs={{0,12},{1,13},{2,14},{3,15},{4,0},{5,1},{6,2},{7,3},{8,4},{9,5},{1... | collective-permute-start | bytes 2457608 | tf_op jit(solution)/shard_map/ppermute | solution.py:33
  55.5 4.6 %copy-start.4 = (bf16[640,512]{0,1:T(8,128)(2,1)}, bf16[640,512]{0,1:T(8,128)(2,1)S(1)}, u32[]{:S(2)}) copy-start(bf16[640,512]{0,1:T(8,128)(2,1)S(1)} %collective-permute-done.4) | copy-start | bytes 1966084
  55.5 37.3 %collective-permute-start.9 = (bf16[640,640]{1,0:T(8,128)(2,1)S(1)}, bf16[640,640]{1,0:T(8,128)(2,1)}, u32[]{:S(2)}, u32[]{:S(2)}) collective-permute-start(bf16[640,640]{1,0:T(8,128)(2,1)S(1)} %collective-permute-done.7), channel_id=1, source_target_pairs={{0,8},{1,9},{2,10},{3,11},{4,12},{5,13},{6,14},{7,15},{8,0},{9,1},... | collective-permute-start | bytes 2457608 | tf_op jit(solution)/shard_map/ppermute | solution.py:33
  60.0 0.9 copy-start.6
  60.9 12.8 %collective-permute-start.11 = (bf16[640,512]{0,1:T(8,128)(2,1)}, bf16[640,512]{0,1:T(8,128)(2,1)}, u32[]{:S(2)}, u32[]{:S(2)}) collective-permute-start(bf16[640,512]{0,1:T(8,128)(2,1)} %pad_maximum_fusion.2), channel_id=1, source_target_pairs={{0,192},{2,194},{4,196},{6,198},{8,200},{10,202},{12,204},{14,206}... | collective-permute-start | bytes 1966088 | tf_op jit(solution)/shard_map/ppermute | solution.py:33
  64.7 34.8 %collective-permute-start.15 = (bf16[640,512]{0,1:T(8,128)(2,1)}, bf16[640,512]{0,1:T(8,128)(2,1)}, u32[]{:S(2)}, u32[]{:S(2)}) collective-permute-start(bf16[640,512]{0,1:T(8,128)(2,1)} %pad_maximum_fusion.2), channel_id=1, source_target_pairs={{0,128},{2,130},{4,132},{6,134},{8,136},{10,138},{12,140},{14,142}... | collective-permute-start | bytes 1966088 | tf_op jit(solution)/shard_map/ppermute | solution.py:33
  73.7 28.9 %collective-permute-start.19 = (bf16[640,512]{0,1:T(8,128)(2,1)}, bf16[640,512]{0,1:T(8,128)(2,1)S(1)}, u32[]{:S(2)}, u32[]{:S(2)}) collective-permute-start(bf16[640,512]{0,1:T(8,128)(2,1)} %pad_maximum_fusion.2), channel_id=1, source_target_pairs={{0,64},{2,66},{4,68},{6,70},{8,72},{10,74},{12,76},{14,78},{17,81}... | collective-permute-start | bytes 1966088 | tf_op jit(solution)/shard_map/ppermute | solution.py:33
  76.6 27.3 %collective-permute-start.12 = (bf16[640,512]{0,1:T(8,128)(2,1)}, bf16[640,512]{0,1:T(8,128)(2,1)S(1)}, u32[]{:S(2)}, u32[]{:S(2)}) collective-permute-start(bf16[640,512]{0,1:T(8,128)(2,1)} %collective-permute-done.11), channel_id=1, source_target_pairs={{0,16},{2,18},{4,20},{6,22},{8,24},{10,26},{12,28},{14,30},{17,33}... | collective-permute-start | bytes 1966088 | tf_op jit(solution)/shard_map/ppermute | solution.py:33
  78.0 28.5 %collective-permute-start.13 = (bf16[640,512]{0,1:T(8,128)(2,1)}, bf16[640,512]{0,1:T(8,128)(2,1)S(1)}, u32[]{:S(2)}, u32[]{:S(2)}) collective-permute-start(bf16[640,512]{0,1:T(8,128)(2,1)} %collective-permute-done.11), channel_id=1, source_target_pairs={{0,48},{2,50},{4,52},{6,54},{8,56},{10,58},{12,60},{14,62},{17,1},... | collective-permute-start | bytes 1966088 | tf_op jit(solution)/shard_map/ppermute | solution.py:33
  92.8 15.1 %collective-permute-start.14 = (bf16[640,512]{0,1:T(8,128)(2,1)}, bf16[640,512]{0,1:T(8,128)(2,1)S(1)}, u32[]{:S(2)}, u32[]{:S(2)}) collective-permute-start(bf16[640,512]{0,1:T(8,128)(2,1)} %collective-permute-done.11), channel_id=1, source_target_pairs={{0,32},{2,34},{4,36},{6,38},{8,40},{10,42},{12,44},{14,46},{17,49}... | collective-permute-start | bytes 1966088 | tf_op jit(solution)/shard_map/ppermute | solution.py:33
  97.6 3.4 %copy-start.5 = (bf16[640,512]{0,1:T(8,128)(2,1)S(1)}, bf16[640,512]{0,1:T(8,128)(2,1)}, u32[]{:S(2)}) copy-start(bf16[640,512]{0,1:T(8,128)(2,1)} %copy-done.4) | copy-start | bytes 1966084
  97.6 3.4 %copy-start.7 = (bf16[640,512]{0,1:T(8,128)(2,1)S(1)}, bf16[640,512]{0,1:T(8,128)(2,1)}, u32[]{:S(2)}) copy-start(bf16[640,512]{0,1:T(8,128)(2,1)} %copy-done.6) | copy-start | bytes 1966084
  99.6 13.4 %collective-permute-start.16 = (bf16[640,512]{0,1:T(8,128)(2,1)}, bf16[640,512]{0,1:T(8,128)(2,1)S(1)}, u32[]{:S(2)}, u32[]{:S(2)}) collective-permute-start(bf16[640,512]{0,1:T(8,128)(2,1)} %collective-permute-done.15), channel_id=1, source_target_pairs={{0,16},{2,18},{4,20},{6,22},{8,24},{10,26},{12,28},{14,30},{17,33}... | collective-permute-start | bytes 1966088 | tf_op jit(solution)/shard_map/ppermute | solution.py:33
  102.6 16.8 %collective-permute-start.17 = (bf16[640,512]{0,1:T(8,128)(2,1)}, bf16[640,512]{0,1:T(8,128)(2,1)S(1)}, u32[]{:S(2)}, u32[]{:S(2)}) collective-permute-start(bf16[640,512]{0,1:T(8,128)(2,1)} %collective-permute-done.15), channel_id=1, source_target_pairs={{0,48},{2,50},{4,52},{6,54},{8,56},{10,58},{12,60},{14,62},{17,1},... | collective-permute-start | bytes 1966088 | tf_op jit(solution)/shard_map/ppermute | solution.py:33
  103.9 17.2 %collective-permute-start.18 = (bf16[640,512]{0,1:T(8,128)(2,1)}, bf16[640,512]{0,1:T(8,128)(2,1)S(1)}, u32[]{:S(2)}, u32[]{:S(2)}) collective-permute-start(bf16[640,512]{0,1:T(8,128)(2,1)} %collective-permute-done.15), channel_id=1, source_target_pairs={{0,32},{2,34},{4,36},{6,38},{8,40},{10,42},{12,44},{14,46},{17,49}... | collective-permute-start | bytes 1966088 | tf_op jit(solution)/shard_map/ppermute | solution.py:33
  106.5 20.5 %collective-permute-start.20 = (bf16[640,512]{0,1:T(8,128)(2,1)S(1)}, bf16[640,512]{0,1:T(8,128)(2,1)S(1)}, u32[]{:S(2)}, u32[]{:S(2)}) collective-permute-start(bf16[640,512]{0,1:T(8,128)(2,1)S(1)} %collective-permute-done.19), channel_id=1, source_target_pairs={{0,16},{2,18},{4,20},{6,22},{8,24},{10,26},{12,28},{14,30},{17,33}... | collective-permute-start | bytes 1966088 | tf_op jit(solution)/shard_map/ppermute | solution.py:33
  107.9 25.4 %collective-permute-start.21 = (bf16[640,512]{0,1:T(8,128)(2,1)S(1)}, bf16[640,512]{0,1:T(8,128)(2,1)S(1)}, u32[]{:S(2)}, u32[]{:S(2)}) collective-permute-start(bf16[640,512]{0,1:T(8,128)(2,1)S(1)} %collective-permute-done.19), channel_id=1, source_target_pairs={{0,48},{2,50},{4,52},{6,54},{8,56},{10,58},{12,60},{14,62},{17,1},... | collective-permute-start | bytes 1966088 | tf_op jit(solution)/shard_map/ppermute | solution.py:33
  113.0 22.1 %collective-permute-start.22 = (bf16[640,512]{0,1:T(8,128)(2,1)S(1)}, bf16[640,512]{0,1:T(8,128)(2,1)S(1)}, u32[]{:S(2)}, u32[]{:S(2)}) collective-permute-start(bf16[640,512]{0,1:T(8,128)(2,1)S(1)} %collective-permute-done.19), channel_id=1, source_target_pairs={{0,32},{2,34},{4,36},{6,38},{8,40},{10,42},{12,44},{14,46},{17,49}... | collective-permute-start | bytes 1966088 | tf_op jit(solution)/shard_map/ppermute | solution.py:33
  136.8 2.2 %collective-permute-start.23 = (f32[640,256]{1,0:T(8,128)S(1)}, f32[640,256]{1,0:T(8,128)S(1)}, u32[]{:S(2)}, u32[]{:S(2)}) collective-permute-start(f32[640,256]{1,0:T(8,128)S(1)} %slice.9), channel_id=1, source_target_pairs={{0,1},{1,0},{2,3},{3,2},{4,5},{5,4},{6,7},{7,6},{8,9},{9,8},{10,11... | collective-permute-start | bytes 1966088 | tf_op jit(solution)/shard_map/ppermute | solution.py:33
  137.2 18.7 %copy-start.8 = (f32[1,16,256]{2,1,0:T(8,128)S(1)}, f32[1,16,256]{2,1,0:T(8,128)}, u32[]{:S(2)}) copy-start(f32[1,16,256]{2,1,0:T(8,128)} %param.6) | copy-start | bytes 49156
  139.2 17.3 %copy-start = (bf16[640,256]{1,0:T(8,128)(2,1)}, bf16[640,256]{1,0:T(8,128)(2,1)S(1)}, u32[]{:S(2)}) copy-start(bf16[640,256]{1,0:T(8,128)(2,1)S(1)} %fusion.31) | copy-start | bytes 983044
where the time goes:
time: 157 us
  starting transfers between devices  61.8 us (39%)
  waiting for transfers between devices  57.4 us (37%)
  blocking collectives  16.4 us (10%)
  matrix products  10.9 us (7%)
  other arithmetic  5.78 us (4%)
  local copies, waits for them, and re-layouts  3.07 us (2%)
    ppermute x24, starting transfers between devices, _move(): return lax.ppermute(value, AXES, pairs)  61.8 us
    ppermute x24, waiting for transfers between devices, _move(): return lax.ppermute(value, AXES, pairs)  57.4 us
    all_to_all x1, blocking collectives, body(): lax.all_to_all(part.reshape(16, cols // 16, cols), ('zl', 'x'), 0, 0)  16.4 us
    dot_general x8, matrix products, body(): product = jnp.dot(block, piece, preferred_element_type=jnp.float32)  10.7 us
    another operation x2, other arithmetic, along_y(): jnp.stack([v, _move(v, lambda zl, x, y, zh, c: (zl, x, y - 1, zh, c)), _m...  3.64 us
  transfers between devices with their start and end apart: 24, of which 12 were waited for; matrix products, arithmetic and copies ran while one was open for 10% of the time, Pallas kernels for 0%

commit v1 on v0

v1 whole, which is shorter than its diff:
```python
import jax
import jax.numpy as jnp
from jax import lax
from jax.sharding import Mesh, PartitionSpec as P


AXES = ("zl", "x", "y", "zh", "core")
SIZES = (4, 4, 4, 2, 2)
PASSED = ('ay',)
KEPT = (1, 2, 3)
DOTS = (('n', 0), ('n', 1), ('n', 3), ('f', 0), ('f', 1), ('f', 3), ('n', 2), ('f', 2))


def _places():
    for zl in range(4):
        for x in range(4):
            for y in range(4):
                for zh in range(2):
                    for core in range(2):
                        yield zl, x, y, zh, core


def _index(place):
    out = 0
    for value, size in zip(place, SIZES):
        out = out * size + value % size
    return out


def _move(value, target, senders=None):
    pairs = [
        (_index(p), _index(target(*p)))
        for p in _places()
        if senders is None or senders(*p)
    ]
    return lax.ppermute(value, AXES, pairs)


def _matched(zl, x, y, zh, core):
    return x % 2 == core


def _unmatched(zl, x, y, zh, core):
    return x % 2 != core


def body(inverse_block, factor_cols, diag_inverse, fill_mask):
    rows, cols = factor_cols.shape
    zl, x, y, zh, core = (lax.axis_index(a) for a in AXES)
    row = zl * 4 + x
    col = y * 4 + zh * 2 + core
    pieces = rows // 128

    halves = jnp.repeat(fill_mask, 2, axis=0)
    mask = lax.dynamic_slice(halves, (row * pieces, col), (pieces, 1)).reshape(pieces, 1, 1)

    def along_y(name, v):
        left = _move(v, lambda zl, x, y, zh, c: (zl, x, y - 1, zh, c))
        if name in PASSED:
            across = _move(left, lambda zl, x, y, zh, c: (zl, x, y - 1, zh, c))
        else:
            across = _move(v, lambda zl, x, y, zh, c: (zl, x, y + 2, zh, c))
        right = _move(v, lambda zl, x, y, zh, c: (zl, x, y + 1, zh, c))
        return jnp.stack([v, left, across, right])

    across_z = lambda zl, x, y, zh, c: (zl, x, y, zh + 1, c)
    near_blocks = along_y("ay", inverse_block)
    far = _move(inverse_block, across_z, _unmatched) + _move(inverse_block, across_z, _matched)
    far_blocks = along_y("by", far)

    selected = (factor_cols.reshape(pieces, 128, cols) * mask.astype(jnp.bfloat16)).reshape(rows, cols)
    other = _move(selected, lambda zl, x, y, zh, c: (zl, x, y, zh, 1 - c),
                  lambda zl, x, y, zh, c: x % 2 != c)
    both = jnp.concatenate([selected, other], axis=1)
    is_matched = (x % 2) == core
    first_near = (jnp.where(is_matched, x, (x + 3) % 4) // 2) == zh
    pairs = []
    for d in range(4):
        v = both
        if d:
            v = _move(both, lambda zl, x, y, zh, c: (zl - d, x, y, zh, c), _matched)
        right = _move(v, lambda zl, x, y, zh, c: (zl, x + 1, y, zh, c), _matched)
        left = _move(v, lambda zl, x, y, zh, c: (zl, x - 1, y, zh, c), _matched)
        if f"r{d}" in PASSED:
            across = _move(right, lambda zl, x, y, zh, c: (zl, x + 1, y, zh, c), _unmatched)
        elif f"l{d}" in PASSED:
            across = _move(left, lambda zl, x, y, zh, c: (zl, x - 1, y, zh, c), _unmatched)
        else:
            across = _move(v, lambda zl, x, y, zh, c: (zl, x + 2, y, zh, c), _matched)
        if d in KEPT:
            v = lax.optimization_barrier(jnp.where(is_matched, v, jnp.zeros_like(v)))
        pairs.append((v, right, left, across))

    total = None
    for near, d in DOTS:
        parts = pairs[d]
        if total is not None:
            total, *parts = lax.optimization_barrier((total, *parts))
        v, right, left, across = parts
        first = jnp.where(is_matched, v, right)
        second = jnp.where(is_matched, across, left)
        piece = jnp.where(first_near == (near == "n"), first, second)
        stack = near_blocks if near == "n" else far_blocks
        block = lax.dynamic_index_in_dim(stack, (zl + d - y) % 4, 0, keepdims=False)
        product = jnp.dot(block, piece, preferred_element_type=jnp.float32)
        total = product if total is None else total + product

    theirs = _move(total[:, cols:], lambda zl, x, y, zh, c: (zl, x, y, zh, 1 - c))
    summed = (total[:, :cols] + theirs).reshape(pieces, 128, cols)
    inverse_cols = (-summed * mask.astype(jnp.float32)).astype(jnp.bfloat16).reshape(rows, cols)

    part = jnp.einsum("ia,ib->ab", selected, inverse_cols, preferred_element_type=jnp.float32)
    shares = lax.all_to_all(part.reshape(16, cols // 16, cols), ("zl", "x"), 0, 0)
    inverse_diag = diag_inverse - jnp.sum(shares, axis=0)[None]
    return inverse_cols, inverse_diag


def solution(mesh):
    fine = Mesh(mesh.devices.reshape(SIZES), AXES)
    row, col = ("zl", "x"), ("y", "zh", "core")
    return jax.shard_map(
        body,
        mesh=fine,
        in_specs=(P(row, col), P(row, col), P(col, row, None), P()),
        out_specs=(P(row, col), P(col, row, None)),
        check_vma=False,
    )
```

time: 157 us -> 170 us (1.083)
  the two profiles are of different devices: /device:TPU:8 before, /device:TPU:1 now
where the time goes in v1:
time: 170 us; the launch traced here: 169 us
  waiting for transfers between devices  80.9 us (48%)
  starting transfers between devices  46 us (27%)
  blocking collectives  22.6 us (13%)
  matrix products  8.49 us (5%)
  other arithmetic  7.27 us (4%)
  local copies, waits for them, and re-layouts  3.05 us (2%)
    ppermute x25, waiting for transfers between devices, _move(): return lax.ppermute(value, AXES, pairs)  80.9 us
    ppermute x25, starting transfers between devices, _move(): return lax.ppermute(value, AXES, pairs)  46 us
    all_to_all x1, blocking collectives, body(): lax.all_to_all(part.reshape(16, cols // 16, cols), ('zl', 'x'), 0, 0)  22.6 us
    dot_general x8, matrix products, body(): product = jnp.dot(block, piece, preferred_element_type=jnp.float32)  8.22 us
  transfers between devices with their start and end apart: 25, of which 10 were waited for; matrix products, arithmetic and copies ran while one was open for 9% of the time, Pallas kernels for 0%

profile of v1, /device:TPU:1, one launch (start us, length us, event | category | flops | bytes accessed | tf_op | source)
XLA Modules:
  0.0 169.4 jit_solution(3618382866581991681)
XLA Ops:
  0.6 2.2 %collective-permute-start.2 = (bf16[640,640]{1,0:T(8,128)(2,1)}, bf16[640,640]{1,0:T(8,128)(2,1)S(1)}, u32[]{:S(2)}, u32[]{:S(2)}) collective-permute-start(bf16[640,640]{1,0:T(8,128)(2,1)} %param.4), channel_id=1, source_target_pairs={{0,4},{1,5},{2,6},{3,7},{4,8},{5,9},{6,10},{7,11},{8,12},{9,13},{1... | collective-permute-start | bytes 2457608 | tf_op jit(solution)/shard_map/ppermute | solution.py:36
  2.8 1.2 copy.10
  4.0 0.8 copy.9
  5.1 3.0 %collective-permute-start.3 = (bf16[640,256]{0,1:T(8,128)(2,1)S(1)}, bf16[640,256]{0,1:T(8,128)(2,1)S(1)}, u32[]{:S(2)}, u32[]{:S(2)}) collective-permute-start(bf16[640,256]{0,1:T(8,128)(2,1)S(1)} %broadcast_multiply_fusion), channel_id=1, source_target_pairs={{1,0},{3,2},{5,4},{7,6},{9,8},{11,10},{13,12},{15,14},{16,17},{18,... | collective-permute-start | bytes 983048 | tf_op jit(solution)/shard_map/ppermute | solution.py:36
  8.1 3.0 %collective-permute-start = (bf16[640,640]{1,0:T(8,128)(2,1)}, bf16[640,640]{1,0:T(8,128)(2,1)S(1)}, u32[]{:S(2)}, u32[]{:S(2)}) collective-permute-start(bf16[640,640]{1,0:T(8,128)(2,1)} %param.4), channel_id=1, source_target_pairs={{0,12},{1,13},{2,14},{3,15},{4,0},{5,1},{6,2},{7,3},{8,4},{9,5},{1... | collective-permute-start | bytes 2457608 | tf_op jit(solution)/shard_map/ppermute | solution.py:36
  11.2 7.1 %collective-permute-start.15 = (bf16[640,640]{1,0:T(8,128)(2,1)}, bf16[640,640]{1,0:T(8,128)(2,1)S(1)}, u32[]{:S(2)}, u32[]{:S(2)}) collective-permute-start(bf16[640,640]{1,0:T(8,128)(2,1)} %param.4), channel_id=1, source_target_pairs={{1,3},{3,1},{5,7},{7,5},{9,11},{11,9},{13,15},{15,13},{16,18},{18,... | collective-permute-start | bytes 2457608 | tf_op jit(solution)/shard_map/ppermute | solution.py:36
  18.3 0.7 collective-permute-start.16
  19.1 0.7 collective-permute-start.5
  19.8 0.7 collective-permute-done.2
  20.5 1.3 collective-permute-start.6
  21.8 7.6 %collective-permute-done = bf16[640,640]{1,0:T(8,128)(2,1)S(1)} collective-permute-done((bf16[640,640]{1,0:T(8,128)(2,1)}, bf16[640,640]{1,0:T(8,128)(2,1)S(1)}, u32[]{:S(2)}, u32[]{:S(2)}) %collective-permute-start) | collective-permute-done | bytes 819232 | tf_op jit(solution)/shard_map/ppermute | solution.py:36
  29.4 1.5 collective-permute-start.7
  30.9 10.3 %collective-permute-done.15 = bf16[640,640]{1,0:T(8,128)(2,1)S(1)} collective-permute-done((bf16[640,640]{1,0:T(8,128)(2,1)}, bf16[640,640]{1,0:T(8,128)(2,1)S(1)}, u32[]{:S(2)}, u32[]{:S(2)}) %collective-permute-start.15) | collective-permute-done | bytes 819232 | tf_op jit(solution)/shard_map/ppermute | solution.py:36
  41.2 1.3 collective-permute-start.4
  42.5 1.5 collective-permute-start.11
  44.0 1.5 collective-permute-start.20
  45.6 0.8 copy-done.9
  46.4 1.6 collective-permute-start.1
  48.1 1.7 add.116
  49.7 1.3 collective-permute-start.8
  51.1 2.7 %collective-permute-done.4 = bf16[640,512]{0,1:T(8,128)(2,1)} collective-permute-done((bf16[640,512]{0,1:T(8,128)(2,1)S(1)}, bf16[640,512]{0,1:T(8,128)(2,1)}, u32[]{:S(2)}, u32[]{:S(2)}) %collective-permute-start.4) | collective-permute-done | bytes 655392 | tf_op jit(solution)/shard_map/ppermute | solution.py:36
  53.8 1.3 collective-permute-start.9
  55.1 0.7 collective-permute-start.10
  55.9 1.3 collective-permute-start.12
  57.3 0.7 collective-permute-done.1
  58.0 1.3 collective-permute-start.13
  59.3 26.3 %collective-permute-done.8 = bf16[640,512]{0,1:T(8,128)(2,1)S(1)} collective-permute-done((bf16[640,512]{0,1:T(8,128)(2,1)}, bf16[640,512]{0,1:T(8,128)(2,1)S(1)}, u32[]{:S(2)}, u32[]{:S(2)}) %collective-permute-start.8) | collective-permute-done | bytes 655392 | tf_op jit(solution)/shard_map/ppermute | solution.py:36
  85.6 0.7 collective-permute-start.14
  86.4 1.6 pad_maximum_fusion
  88.1 1.8 %collective-permute-start.18 = (bf16[640,640]{1,0:T(8,128)(2,1)S(1)}, bf16[640,640]{1,0:T(8,128)(2,1)S(1)}, u32[]{:S(2)}, u32[]{:S(2)}) collective-permute-start(bf16[640,640]{1,0:T(8,128)(2,1)S(1)} %add.116), channel_id=1, source_target_pairs={{0,8},{1,9},{2,10},{3,11},{4,12},{5,13},{6,14},{7,15},{8,0},{9,1},... | collective-permute-start | bytes 2457608 | tf_op jit(solution)/shard_map/ppermute | solution.py:36
  89.9 11.8 %collective-permute-done.12 = bf16[640,512]{0,1:T(8,128)(2,1)S(1)} collective-permute-done((bf16[640,512]{0,1:T(8,128)(2,1)}, bf16[640,512]{0,1:T(8,128)(2,1)S(1)}, u32[]{:S(2)}, u32[]{:S(2)}) %collective-permute-start.12) | collective-permute-done | bytes 655392 | tf_op jit(solution)/shard_map/ppermute | solution.py:36
  102.2 1.9 %fusion.14 = f32[640,512]{1,0:T(8,128)S(1)} fusion(bf16[4,640,640]{2,1,0:T(8,128)(2,1)S(1)} %pad_maximum_fusion, s32[]{:T(128)S(6)} %select_n.182, bf16[640,512]{0,1:T(8,128)(2,1)S(1)} %copy-done.8, bf16[640,512]{0,1:T(8,128)(2,1)S(1)} %copy-done.10, bf16[640,512]{0,1:T(8,128)(2,1)} %collective-permute-done.4, pred[]{:T(512)S(6)} %eq.23, pred[]{:T(512)S(6)} %eq.24, ...), kind=kOutput, calls=%fused_computation.16 | convolution fusion | flops 421724160 | bytes 4751366 | tf_op jit(solution)/shard_map/dot_general | solution.py:105
  104.2 0.7 fusion.12
  105.2 1.3 collective-permute-start.21
  106.5 1.3 collective-permute-start.22
  107.8 0.7 fusion.10
  108.9 0.9 collective-permute-start.23
  109.7 4.7 %collective-permute-done.18 = bf16[640,640]{1,0:T(8,128)(2,1)S(1)} collective-permute-done((bf16[640,640]{1,0:T(8,128)(2,1)S(1)}, bf16[640,640]{1,0:T(8,128)(2,1)S(1)}, u32[]{:S(2)}, u32[]{:S(2)}) %collective-permute-start.18) | collective-permute-done | bytes 819232 | tf_op jit(solution)/shard_map/ppermute | solution.py:36
  114.5 14.4 %collective-permute-done.17 = bf16[640,640]{1,0:T(8,128)(2,1)S(1)} collective-permute-done((bf16[640,640]{1,0:T(8,128)(2,1)S(1)}, bf16[640,640]{1,0:T(8,128)(2,1)S(1)}, u32[]{:S(2)}, u32[]{:S(2)}) %collective-permute-start.17) | collective-permute-done | bytes 819232 | tf_op jit(solution)/shard_map/ppermute | solution.py:36
  129.4 1.9 %fusion.8 = f32[640,512]{1,0:T(8,128)S(1)} fusion(bf16[4,640,640]{2,1,0:T(8,128)(2,1)S(1)} %pad_maximum_fusion.1, s32[]{:T(128)S(6)} %select_n.182, bf16[640,512]{0,1:T(8,128)(2,1)S(1)} %copy-done.8, bf16[640,512]{0,1:T(8,128)(2,1)S(1)} %copy-done.10, bf16[640,512]{0,1:T(8,128)(2,1)S(1)} %pad_maximum_fusion.2, bf16[640,512]{0,1:T(8,128)(2,1)} %collective-permute-done.4, ...), kind=kOutput, calls=%fused_computation.10 | convolution fusion | flops 420413440 | bytes 4751366 | tf_op jit(solution)/shard_map/dot_general | solution.py:105
  131.6 0.7 fusion.6
  132.6 0.7 fusion.4
  133.7 0.7 fusion.2
  134.7 0.7 fusion
  135.8 8.1 %collective-permute-start.24 = (f32[640,256]{1,0:T(8,128)S(1)}, f32[640,256]{1,0:T(8,128)S(1)}, u32[]{:S(2)}, u32[]{:S(2)}) collective-permute-start(f32[640,256]{1,0:T(8,128)S(1)} %slice.9), channel_id=1, source_target_pairs={{0,1},{1,0},{2,3},{3,2},{4,5},{5,4},{6,7},{7,6},{8,9},{9,8},{10,11... | collective-permute-start | bytes 1966088 | tf_op jit(solution)/shard_map/ppermute | solution.py:36
  144.2 1.5 collective-permute-done.24
  146.2 22.6 %all_to_all.5 = f32[16,16,256]{2,1,0:T(8,128)S(1)} all-to-all(f32[16,16,256]{2,1,0:T(8,128)S(1)} %fusion.67), channel_id=1, replica_groups=mesh['zl'=4,'x'=4,'y'=4,'zh'=2,'core'=2] {'zl','x'}, dimensions={0} | all-to-all | bytes 524288 | tf_op jit(solution)/shard_map/all_to_all | solution.py:113
  168.8 0.6 bitcast_subtract_fusion
  (60 shorter events, 4.5 us)
Async XLA Ops:
  0.6 19.9 %collective-permute-start.2 = (bf16[640,640]{1,0:T(8,128)(2,1)}, bf16[640,640]{1,0:T(8,128)(2,1)S(1)}, u32[]{:S(2)}, u32[]{:S(2)}) collective-permute-start(bf16[640,640]{1,0:T(8,128)(2,1)} %param.4), channel_id=1, source_target_pairs={{0,4},{1,5},{2,6},{3,7},{4,8},{5,9},{6,10},{7,11},{8,12},{9,13},{1... | collective-permute-start | bytes 2457608 | tf_op jit(solution)/shard_map/ppermute | solution.py:36
  5.1 13.9 %collective-permute-start.3 = (bf16[640,256]{0,1:T(8,128)(2,1)S(1)}, bf16[640,256]{0,1:T(8,128)(2,1)S(1)}, u32[]{:S(2)}, u32[]{:S(2)}) collective-permute-start(bf16[640,256]{0,1:T(8,128)(2,1)S(1)} %broadcast_multiply_fusion), channel_id=1, source_target_pairs={{1,0},{3,2},{5,4},{7,6},{9,8},{11,10},{13,12},{15,14},{16,17},{18,... | collective-permute-start | bytes 983048 | tf_op jit(solution)/shard_map/ppermute | solution.py:36
  8.1 21.2 %collective-permute-start = (bf16[640,640]{1,0:T(8,128)(2,1)}, bf16[640,640]{1,0:T(8,128)(2,1)S(1)}, u32[]{:S(2)}, u32[]{:S(2)}) collective-permute-start(bf16[640,640]{1,0:T(8,128)(2,1)} %param.4), channel_id=1, source_target_pairs={{0,12},{1,13},{2,14},{3,15},{4,0},{5,1},{6,2},{7,3},{8,4},{9,5},{1... | collective-permute-start | bytes 2457608 | tf_op jit(solution)/shard_map/ppermute | solution.py:36
  11.2 30.1 %collective-permute-start.15 = (bf16[640,640]{1,0:T(8,128)(2,1)}, bf16[640,640]{1,0:T(8,128)(2,1)S(1)}, u32[]{:S(2)}, u32[]{:S(2)}) collective-permute-start(bf16[640,640]{1,0:T(8,128)(2,1)} %param.4), channel_id=1, source_target_pairs={{1,3},{3,1},{5,7},{7,5},{9,11},{11,9},{13,15},{15,13},{16,18},{18,... | collective-permute-start | bytes 2457608 | tf_op jit(solution)/shard_map/ppermute | solution.py:36
  18.3 24.2 %collective-permute-start.16 = (bf16[640,640]{1,0:T(8,128)(2,1)}, bf16[640,640]{1,0:T(8,128)(2,1)S(1)}, u32[]{:S(2)}, u32[]{:S(2)}) collective-permute-start(bf16[640,640]{1,0:T(8,128)(2,1)} %param.4), channel_id=1, source_target_pairs={{0,2},{2,0},{4,6},{6,4},{8,10},{10,8},{12,14},{14,12},{17,19},{19,... | collective-permute-start | bytes 2457608 | tf_op jit(solution)/shard_map/ppermute | solution.py:36
  19.0 26.6 %copy-start.4 = (bf16[640,256]{0,1:T(8,128)(2,1)}, bf16[640,256]{0,1:T(8,128)(2,1)S(1)}, u32[]{:S(2)}) copy-start(bf16[640,256]{0,1:T(8,128)(2,1)S(1)} %collective-permute-done.3) | copy-start | bytes 983044
  19.1 25.0 %collective-permute-start.5 = (bf16[640,512]{0,1:T(8,128)(2,1)S(1)}, bf16[640,512]{0,1:T(8,128)(2,1)S(1)}, u32[]{:S(2)}, u32[]{:S(2)}) collective-permute-start(bf16[640,512]{0,1:T(8,128)(2,1)S(1)} %pad_maximum_fusion.2), channel_id=1, source_target_pairs={{0,32},{2,34},{4,36},{6,38},{8,40},{10,42},{12,44},{14,46},{17,49}... | collective-permute-start | bytes 1966088 | tf_op jit(solution)/shard_map/ppermute | solution.py:36
  20.5 25.1 %collective-permute-start.6 = (bf16[640,512]{0,1:T(8,128)(2,1)S(1)}, bf16[640,512]{0,1:T(8,128)(2,1)S(1)}, u32[]{:S(2)}, u32[]{:S(2)}) collective-permute-start(bf16[640,512]{0,1:T(8,128)(2,1)S(1)} %pad_maximum_fusion.2), channel_id=1, source_target_pairs={{0,48},{2,50},{4,52},{6,54},{8,56},{10,58},{12,60},{14,62},{17,1},... | collective-permute-start | bytes 1966088 | tf_op jit(solution)/shard_map/ppermute | solution.py:36
  29.4 20.4 %collective-permute-start.7 = (bf16[640,512]{0,1:T(8,128)(2,1)S(1)}, bf16[640,512]{0,1:T(8,128)(2,1)}, u32[]{:S(2)}, u32[]{:S(2)}) collective-permute-start(bf16[640,512]{0,1:T(8,128)(2,1)S(1)} %pad_maximum_fusion.2), channel_id=1, source_target_pairs={{0,192},{2,194},{4,196},{6,198},{8,200},{10,202},{12,204},{14,206}... | collective-permute-start | bytes 1966088 | tf_op jit(solution)/shard_map/ppermute | solution.py:36
  41.2 4.3 %copy-start.2 = (bf16[640,640]{1,0:T(8,128)(2,1)}, bf16[640,640]{1,0:T(8,128)(2,1)S(1)}, u32[]{:S(2)}) copy-start(bf16[640,640]{1,0:T(8,128)(2,1)S(1)} %collective-permute-done.15) | copy-start | bytes 2457604
  41.2 12.6 %collective-permute-start.4 = (bf16[640,512]{0,1:T(8,128)(2,1)S(1)}, bf16[640,512]{0,1:T(8,128)(2,1)}, u32[]{:S(2)}, u32[]{:S(2)}) collective-permute-start(bf16[640,512]{0,1:T(8,128)(2,1)S(1)} %pad_maximum_fusion.2), channel_id=1, source_target_pairs={{0,16},{2,18},{4,20},{6,22},{8,24},{10,26},{12,28},{14,30},{17,33}... | collective-permute-start | bytes 1966088 | tf_op jit(solution)/shard_map/ppermute | solution.py:36
  42.5 3.1 %copy-start.3 = (bf16[640,640]{1,0:T(8,128)(2,1)}, bf16[640,640]{1,0:T(8,128)(2,1)S(1)}, u32[]{:S(2)}) copy-start(bf16[640,640]{1,0:T(8,128)(2,1)S(1)} %collective-permute-done.16) | copy-start | bytes 2457604
  42.5 12.6 %collective-permute-start.11 = (bf16[640,512]{0,1:T(8,128)(2,1)S(1)}, bf16[640,512]{0,1:T(8,128)(2,1)}, u32[]{:S(2)}, u32[]{:S(2)}) collective-permute-start(bf16[640,512]{0,1:T(8,128)(2,1)S(1)} %pad_maximum_fusion.2), channel_id=1, source_target_pairs={{0,64},{2,66},{4,68},{6,70},{8,72},{10,74},{12,76},{14,78},{17,81}... | collective-permute-start | bytes 1966088 | tf_op jit(solution)/shard_map/ppermute | solution.py:36
  44.0 1.5 copy-start.7
  44.0 11.8 %collective-permute-start.20 = (bf16[640,512]{0,1:T(8,128)(2,1)S(1)}, bf16[640,512]{0,1:T(8,128)(2,1)}, u32[]{:S(2)}, u32[]{:S(2)}) collective-permute-start(bf16[640,512]{0,1:T(8,128)(2,1)S(1)} %pad_maximum_fusion.2), channel_id=1, source_target_pairs={{0,128},{2,130},{4,132},{6,134},{8,136},{10,138},{12,140},{14,142}... | collective-permute-start | bytes 1966088 | tf_op jit(solution)/shard_map/ppermute | solution.py:36
  45.6 0.8 copy-start.9
  46.4 11.6 %collective-permute-start.1 = (bf16[640,640]{1,0:T(8,128)(2,1)S(1)}, bf16[640,640]{1,0:T(8,128)(2,1)}, u32[]{:S(2)}, u32[]{:S(2)}) collective-permute-start(bf16[640,640]{1,0:T(8,128)(2,1)S(1)} %collective-permute-done), channel_id=1, source_target_pairs={{0,12},{1,13},{2,14},{3,15},{4,0},{5,1},{6,2},{7,3},{8,4},{9,5},{1... | collective-permute-start | bytes 2457608 | tf_op jit(solution)/shard_map/ppermute | solution.py:36
  48.1 38.3 %copy-start.1 = (bf16[640,640]{1,0:T(8,128)(2,1)S(1)}, bf16[640,640]{1,0:T(8,128)(2,1)}, u32[]{:S(2)}) copy-start(bf16[640,640]{1,0:T(8,128)(2,1)} %param.4) | copy-start | bytes 2457604
  49.7 35.9 %collective-permute-start.8 = (bf16[640,512]{0,1:T(8,128)(2,1)}, bf16[640,512]{0,1:T(8,128)(2,1)S(1)}, u32[]{:S(2)}, u32[]{:S(2)}) collective-permute-start(bf16[640,512]{0,1:T(8,128)(2,1)} %collective-permute-done.7), channel_id=1, source_target_pairs={{0,16},{2,18},{4,20},{6,22},{8,24},{10,26},{12,28},{14,30},{17,33}... | collective-permute-start | bytes 1966088 | tf_op jit(solution)/shard_map/ppermute | solution.py:36
  53.8 34.2 %collective-permute-start.9 = (bf16[640,512]{0,1:T(8,128)(2,1)}, bf16[640,512]{0,1:T(8,128)(2,1)S(1)}, u32[]{:S(2)}, u32[]{:S(2)}) collective-permute-start(bf16[640,512]{0,1:T(8,128)(2,1)} %collective-permute-done.7), channel_id=1, source_target_pairs={{0,48},{2,50},{4,52},{6,54},{8,56},{10,58},{12,60},{14,62},{17,1},... | collective-permute-start | bytes 1966088 | tf_op jit(solution)/shard_map/ppermute | solution.py:36
  55.1 33.0 %collective-permute-start.10 = (bf16[640,512]{0,1:T(8,128)(2,1)}, bf16[640,512]{0,1:T(8,128)(2,1)S(1)}, u32[]{:S(2)}, u32[]{:S(2)}) collective-permute-start(bf16[640,512]{0,1:T(8,128)(2,1)} %collective-permute-done.7), channel_id=1, source_target_pairs={{0,32},{2,34},{4,36},{6,38},{8,40},{10,42},{12,44},{14,46},{17,49}... | collective-permute-start | bytes 1966088 | tf_op jit(solution)/shard_map/ppermute | solution.py:36
  55.9 45.9 %collective-permute-start.12 = (bf16[640,512]{0,1:T(8,128)(2,1)}, bf16[640,512]{0,1:T(8,128)(2,1)S(1)}, u32[]{:S(2)}, u32[]{:S(2)}) collective-permute-start(bf16[640,512]{0,1:T(8,128)(2,1)} %collective-permute-done.11), channel_id=1, source_target_pairs={{0,16},{2,18},{4,20},{6,22},{8,24},{10,26},{12,28},{14,30},{17,33}... | collective-permute-start | bytes 1966088 | tf_op jit(solution)/shard_map/ppermute | solution.py:36
  58.0 47.2 %collective-permute-start.13 = (bf16[640,512]{0,1:T(8,128)(2,1)}, bf16[640,512]{0,1:T(8,128)(2,1)S(1)}, u32[]{:S(2)}, u32[]{:S(2)}) collective-permute-start(bf16[640,512]{0,1:T(8,128)(2,1)} %collective-permute-done.11), channel_id=1, source_target_pairs={{0,48},{2,50},{4,52},{6,54},{8,56},{10,58},{12,60},{14,62},{17,1},... | collective-permute-start | bytes 1966088 | tf_op jit(solution)/shard_map/ppermute | solution.py:36
  85.6 20.9 %collective-permute-start.14 = (bf16[640,512]{0,1:T(8,128)(2,1)}, bf16[640,512]{0,1:T(8,128)(2,1)S(1)}, u32[]{:S(2)}, u32[]{:S(2)}) collective-permute-start(bf16[640,512]{0,1:T(8,128)(2,1)} %collective-permute-done.11), channel_id=1, source_target_pairs={{0,32},{2,34},{4,36},{6,38},{8,40},{10,42},{12,44},{14,46},{17,49}... | collective-permute-start | bytes 1966088 | tf_op jit(solution)/shard_map/ppermute | solution.py:36
  86.4 15.9 %copy-start.5 = (bf16[640,256]{0,1:T(8,128)(2,1)S(1)}, bf16[640,256]{0,1:T(8,128)(2,1)}, u32[]{:S(2)}) copy-start(bf16[640,256]{0,1:T(8,128)(2,1)} %copy-done.4) | copy-start | bytes 983044
  86.4 15.9 %copy-start.8 = (bf16[640,512]{0,1:T(8,128)(2,1)S(1)}, bf16[640,512]{0,1:T(8,128)(2,1)}, u32[]{:S(2)}) copy-start(bf16[640,512]{0,1:T(8,128)(2,1)} %copy-done.7) | copy-start | bytes 1966084
  86.4 15.9 %copy-start.10 = (bf16[640,512]{0,1:T(8,128)(2,1)S(1)}, bf16[640,512]{0,1:T(8,128)(2,1)}, u32[]{:S(2)}) copy-start(bf16[640,512]{0,1:T(8,128)(2,1)} %copy-done.9) | copy-start | bytes 1966084
  88.0 20.8 %collective-permute-start.19 = (bf16[640,640]{1,0:T(8,128)(2,1)S(1)}, bf16[640,640]{1,0:T(8,128)(2,1)S(1)}, u32[]{:S(2)}, u32[]{:S(2)}) collective-permute-start(bf16[640,640]{1,0:T(8,128)(2,1)S(1)} %add.116), channel_id=1, source_target_pairs={{0,4},{1,5},{2,6},{3,7},{4,8},{5,9},{6,10},{7,11},{8,12},{9,13},{1... | collective-permute-start | bytes 2457608 | tf_op jit(solution)/shard_map/ppermute | solution.py:36
  88.1 26.3 %collective-permute-start.18 = (bf16[640,640]{1,0:T(8,128)(2,1)S(1)}, bf16[640,640]{1,0:T(8,128)(2,1)S(1)}, u32[]{:S(2)}, u32[]{:S(2)}) collective-permute-start(bf16[640,640]{1,0:T(8,128)(2,1)S(1)} %add.116), channel_id=1, source_target_pairs={{0,8},{1,9},{2,10},{3,11},{4,12},{5,13},{6,14},{7,15},{8,0},{9,1},... | collective-permute-start | bytes 2457608 | tf_op jit(solution)/shard_map/ppermute | solution.py:36
  101.8 27.1 %collective-permute-start.17 = (bf16[640,640]{1,0:T(8,128)(2,1)S(1)}, bf16[640,640]{1,0:T(8,128)(2,1)S(1)}, u32[]{:S(2)}, u32[]{:S(2)}) collective-permute-start(bf16[640,640]{1,0:T(8,128)(2,1)S(1)} %add.116), channel_id=1, source_target_pairs={{0,12},{1,13},{2,14},{3,15},{4,0},{5,1},{6,2},{7,3},{8,4},{9,5},{1... | collective-permute-start | bytes 2457608 | tf_op jit(solution)/shard_map/ppermute | solution.py:36
  105.2 28.4 %collective-permute-start.21 = (bf16[640,512]{0,1:T(8,128)(2,1)}, bf16[640,512]{0,1:T(8,128)(2,1)S(1)}, u32[]{:S(2)}, u32[]{:S(2)}) collective-permute-start(bf16[640,512]{0,1:T(8,128)(2,1)} %collective-permute-done.20), channel_id=1, source_target_pairs={{0,16},{2,18},{4,20},{6,22},{8,24},{10,26},{12,28},{14,30},{17,33}... | collective-permute-start | bytes 1966088 | tf_op jit(solution)/shard_map/ppermute | solution.py:36
  106.5 27.1 %collective-permute-start.22 = (bf16[640,512]{0,1:T(8,128)(2,1)}, bf16[640,512]{0,1:T(8,128)(2,1)S(1)}, u32[]{:S(2)}, u32[]{:S(2)}) collective-permute-start(bf16[640,512]{0,1:T(8,128)(2,1)} %collective-permute-done.20), channel_id=1, source_target_pairs={{0,48},{2,50},{4,52},{6,54},{8,56},{10,58},{12,60},{14,62},{17,1},... | collective-permute-start | bytes 1966088 | tf_op jit(solution)/shard_map/ppermute | solution.py:36
  108.9 24.8 %collective-permute-start.23 = (bf16[640,512]{0,1:T(8,128)(2,1)}, bf16[640,512]{0,1:T(8,128)(2,1)S(1)}, u32[]{:S(2)}, u32[]{:S(2)}) collective-permute-start(bf16[640,512]{0,1:T(8,128)(2,1)} %collective-permute-done.20), channel_id=1, source_target_pairs={{0,32},{2,34},{4,36},{6,38},{8,40},{10,42},{12,44},{14,46},{17,49}... | collective-permute-start | bytes 1966088 | tf_op jit(solution)/shard_map/ppermute | solution.py:36
  135.7 33.1 %copy-start.6 = (f32[1,16,256]{2,1,0:T(8,128)S(1)}, f32[1,16,256]{2,1,0:T(8,128)}, u32[]{:S(2)}) copy-start(f32[1,16,256]{2,1,0:T(8,128)} %param.6) | copy-start | bytes 49156
  135.8 9.9 %collective-permute-start.24 = (f32[640,256]{1,0:T(8,128)S(1)}, f32[640,256]{1,0:T(8,128)S(1)}, u32[]{:S(2)}, u32[]{:S(2)}) collective-permute-start(f32[640,256]{1,0:T(8,128)S(1)} %slice.9), channel_id=1, source_target_pairs={{0,1},{1,0},{2,3},{3,2},{4,5},{5,4},{6,7},{7,6},{8,9},{9,8},{10,11... | collective-permute-start | bytes 1966088 | tf_op jit(solution)/shard_map/ppermute | solution.py:36
  145.9 23.6 %copy-start = (bf16[640,256]{1,0:T(8,128)(2,1)}, bf16[640,256]{1,0:T(8,128)(2,1)S(1)}, u32[]{:S(2)}) copy-start(bf16[640,256]{1,0:T(8,128)(2,1)S(1)} %fusion.26) | copy-start | bytes 983044

commit v2 on v1

--- a/solution.py
+++ b/solution.py
@@ -7,7 +7,7 @@
 AXES = ("zl", "x", "y", "zh", "core")
 SIZES = (4, 4, 4, 2, 2)
 PASSED = ('ay',)
-KEPT = (1, 2, 3)
+KEPT = (2, 3)
 DOTS = (('n', 0), ('n', 1), ('n', 3), ('f', 0), ('f', 1), ('f', 3), ('n', 2), ('f', 2))
 
 
@@ -65,7 +65,9 @@
 
     across_z = lambda zl, x, y, zh, c: (zl, x, y, zh + 1, c)
     near_blocks = along_y("ay", inverse_block)
-    far = _move(inverse_block, across_z, _unmatched) + _move(inverse_block, across_z, _matched)
+    from_unmatched = _move(inverse_block, across_z, _unmatched)
+    from_matched = _move(inverse_block, across_z, _matched)
+    far = jnp.where((x % 2) == core, from_matched, from_unmatched)
     far_blocks = along_y("by", far)
 
     selected = (factor_cols.reshape(pieces, 128, cols) * mask.astype(jnp.bfloat16)).reshape(rows, cols)
@@ -110,8 +112,8 @@
     inverse_cols = (-summed * mask.astype(jnp.float32)).astype(jnp.bfloat16).reshape(rows, cols)
 
     part = jnp.einsum("ia,ib->ab", selected, inverse_cols, preferred_element_type=jnp.float32)
-    shares = lax.all_to_all(part.reshape(16, cols // 16, cols), ("zl", "x"), 0, 0)
-    inverse_diag = diag_inverse - jnp.sum(shares, axis=0)[None]
+    shares = lax.all_to_all(part.astype(jnp.bfloat16).reshape(16, cols // 16, cols), ("zl", "x"), 0, 0)
+    inverse_diag = diag_inverse - jnp.sum(shares.astype(jnp.float32), axis=0)[None]
     return inverse_cols, inverse_diag
 
 

time: 170 us -> 165 us (0.971)
  the two profiles are of different devices: /device:TPU:1 before, /device:TPU:24 now
where the time goes in v2:
time: 165 us; the launch traced here: 164 us
  starting transfers between devices  87.1 us (53%)
  waiting for transfers between devices  31.9 us (19%)
  blocking collectives  24.1 us (15%)
  other arithmetic  9.99 us (6%)
  matrix products  8.27 us (5%)
  local copies, waits for them, and re-layouts  1.88 us (1%)
    ppermute x25, starting transfers between devices, _move(): return lax.ppermute(value, AXES, pairs)  87.1 us
    ppermute x25, waiting for transfers between devices, _move(): return lax.ppermute(value, AXES, pairs)  31.9 us
    all_to_all x1, blocking collectives, body(): lax.all_to_all(part.astype(jnp.bfloat16).reshape(16, cols // 16, cols), (...  24.1 us
    dot_general x8, matrix products, body(): product = jnp.dot(block, piece, preferred_element_type=jnp.float32)  7.96 us
  transfers between devices with their start and end apart: 25, of which 7 were waited for; matrix products, arithmetic and copies ran while one was open for 10% of the time, Pallas kernels for 0%

profile of v2, /device:TPU:24, one launch (start us, length us, event | category | flops | bytes accessed | tf_op | source)
XLA Modules:
  0.0 164.4 jit_solution(11354663160590115091)
XLA Ops:
  0.6 0.8 collective-permute-start
  1.4 0.8 copy.7
  2.5 1.1 broadcast_multiply_fusion
  3.7 1.4 collective-permute-start.3
  5.1 2.6 %collective-permute-start.2 = (bf16[640,640]{1,0:T(8,128)(2,1)}, bf16[640,640]{1,0:T(8,128)(2,1)S(1)}, u32[]{:S(2)}, u32[]{:S(2)}) collective-permute-start(bf16[640,640]{1,0:T(8,128)(2,1)} %param.4), channel_id=1, source_target_pairs={{0,4},{1,5},{2,6},{3,7},{4,8},{5,9},{6,10},{7,11},{8,12},{9,13},{1... | collective-permute-start | bytes 2457608 | tf_op jit(solution)/shard_map/ppermute | solution.py:36
  7.7 9.1 %collective-permute-start.15 = (bf16[640,640]{1,0:T(8,128)(2,1)}, bf16[640,640]{1,0:T(8,128)(2,1)S(1)}, u32[]{:S(2)}, u32[]{:S(2)}) collective-permute-start(bf16[640,640]{1,0:T(8,128)(2,1)} %param.4), channel_id=1, source_target_pairs={{0,2},{2,0},{4,6},{6,4},{8,10},{10,8},{12,14},{14,12},{17,19},{19,... | collective-permute-start | bytes 2457608 | tf_op jit(solution)/shard_map/ppermute | solution.py:36
  16.8 0.7 collective-permute-start.16
  17.5 3.6 %collective-permute-start.4 = (bf16[640,512]{1,0:T(8,128)(2,1)S(1)}, bf16[640,512]{1,0:T(8,128)(2,1)S(1)}, u32[]{:S(2)}, u32[]{:S(2)}) collective-permute-start(bf16[640,512]{1,0:T(8,128)(2,1)S(1)} %pad_maximum_fusion.2), channel_id=1, source_target_pairs={{0,16},{2,18},{4,20},{6,22},{8,24},{10,26},{12,28},{14,30},{17,33}... | collective-permute-start | bytes 1966088 | tf_op jit(solution)/shard_map/ppermute | solution.py:36
  21.2 0.9 collective-permute-done
  22.1 4.9 %collective-permute-start.5 = (bf16[640,512]{1,0:T(8,128)(2,1)S(1)}, bf16[640,512]{1,0:T(8,128)(2,1)S(1)}, u32[]{:S(2)}, u32[]{:S(2)}) collective-permute-start(bf16[640,512]{1,0:T(8,128)(2,1)S(1)} %pad_maximum_fusion.2), channel_id=1, source_target_pairs={{0,32},{2,34},{4,36},{6,38},{8,40},{10,42},{12,44},{14,46},{17,49}... | collective-permute-start | bytes 1966088 | tf_op jit(solution)/shard_map/ppermute | solution.py:36
  27.1 6.5 %collective-permute-start.7 = (bf16[640,512]{1,0:T(8,128)(2,1)S(1)}, bf16[640,512]{1,0:T(8,128)(2,1)}, u32[]{:S(2)}, u32[]{:S(2)}) collective-permute-start(bf16[640,512]{1,0:T(8,128)(2,1)S(1)} %pad_maximum_fusion.2), channel_id=1, source_target_pairs={{0,192},{2,194},{4,196},{6,198},{8,200},{10,202},{12,204},{14,206}... | collective-permute-start | bytes 1966088 | tf_op jit(solution)/shard_map/ppermute | solution.py:36
  33.6 6.1 %collective-permute-done.15 = bf16[640,640]{1,0:T(8,128)(2,1)S(1)} collective-permute-done((bf16[640,640]{1,0:T(8,128)(2,1)}, bf16[640,640]{1,0:T(8,128)(2,1)S(1)}, u32[]{:S(2)}, u32[]{:S(2)}) %collective-permute-start.15) | collective-permute-done | bytes 819232 | tf_op jit(solution)/shard_map/ppermute | solution.py:36
  39.7 2.1 %collective-permute-start.6 = (bf16[640,512]{1,0:T(8,128)(2,1)S(1)}, bf16[640,512]{1,0:T(8,128)(2,1)}, u32[]{:S(2)}, u32[]{:S(2)}) collective-permute-start(bf16[640,512]{1,0:T(8,128)(2,1)S(1)} %pad_maximum_fusion.2), channel_id=1, source_target_pairs={{0,48},{2,50},{4,52},{6,54},{8,56},{10,58},{12,60},{14,62},{17,1},... | collective-permute-start | bytes 1966088 | tf_op jit(solution)/shard_map/ppermute | solution.py:36
  41.9 16.0 %collective-permute-start.11 = (bf16[640,512]{1,0:T(8,128)(2,1)S(1)}, bf16[640,512]{1,0:T(8,128)(2,1)}, u32[]{:S(2)}, u32[]{:S(2)}) collective-permute-start(bf16[640,512]{1,0:T(8,128)(2,1)S(1)} %pad_maximum_fusion.2), channel_id=1, source_target_pairs={{0,64},{2,66},{4,68},{6,70},{8,72},{10,74},{12,76},{14,78},{17,81}... | collective-permute-start | bytes 1966088 | tf_op jit(solution)/shard_map/ppermute | solution.py:36
  57.8 10.5 %collective-permute-start.20 = (bf16[640,512]{1,0:T(8,128)(2,1)S(1)}, bf16[640,512]{1,0:T(8,128)(2,1)}, u32[]{:S(2)}, u32[]{:S(2)}) collective-permute-start(bf16[640,512]{1,0:T(8,128)(2,1)S(1)} %pad_maximum_fusion.2), channel_id=1, source_target_pairs={{0,128},{2,130},{4,132},{6,134},{8,136},{10,138},{12,140},{14,142}... | collective-permute-start | bytes 1966088 | tf_op jit(solution)/shard_map/ppermute | solution.py:36
  68.4 0.8 copy-done.9
  69.2 4.9 %collective-permute-start.10 = (bf16[640,512]{1,0:T(8,128)(2,1)}, bf16[640,512]{1,0:T(8,128)(2,1)S(1)}, u32[]{:S(2)}, u32[]{:S(2)}) collective-permute-start(bf16[640,512]{1,0:T(8,128)(2,1)} %collective-permute-done.7), channel_id=1, source_target_pairs={{0,32},{2,34},{4,36},{6,38},{8,40},{10,42},{12,44},{14,46},{17,49}... | collective-permute-start | bytes 1966088 | tf_op jit(solution)/shard_map/ppermute | solution.py:36
  74.1 1.2 broadcast_select_fusion
  75.4 1.3 collective-permute-start.8
  76.8 1.3 collective-permute-start.9
  78.1 5.9 %collective-permute-done.20 = bf16[640,512]{1,0:T(8,128)(2,1)} collective-permute-done((bf16[640,512]{1,0:T(8,128)(2,1)S(1)}, bf16[640,512]{1,0:T(8,128)(2,1)}, u32[]{:S(2)}, u32[]{:S(2)}) %collective-permute-start.20) | collective-permute-done | bytes 655392 | tf_op jit(solution)/shard_map/ppermute | solution.py:36
  84.0 1.3 collective-permute-start.12
  85.3 1.1 broadcast_select_fusion.2
  86.5 1.1 broadcast_select_fusion.1
  87.6 1.3 collective-permute-start.13
  89.0 4.9 %collective-permute-start.14 = (bf16[640,512]{1,0:T(8,128)(2,1)}, bf16[640,512]{1,0:T(8,128)(2,1)S(1)}, u32[]{:S(2)}, u32[]{:S(2)}) collective-permute-start(bf16[640,512]{1,0:T(8,128)(2,1)} %collective-permute-done.11), channel_id=1, source_target_pairs={{0,32},{2,34},{4,36},{6,38},{8,40},{10,42},{12,44},{14,46},{17,49}... | collective-permute-start | bytes 1966088 | tf_op jit(solution)/shard_map/ppermute | solution.py:36
  94.0 1.6 %pad_maximum_fusion = bf16[4,640,640]{2,1,0:T(8,128)(2,1)S(1)} fusion(bf16[1,640,640]{2,1,0:T(8,128)(2,1)S(1)} %bitcast.45, bf16[1,640,640]{2,1,0:T(8,128)(2,1)} %bitcast.2, bf16[1,640,640]{2,1,0:T(8,128)(2,1)S(1)} %bitcast.44, bf16[1,640,640]{2,1,0:T(8,128)(2,1)S(1)} %bitcast.43), kind=kLoop, calls=%fused_computation | loop fusion | flops 4915200 | bytes 6553600 | tf_op jit(solution)/shard_map/stack | solution.py:64
  95.7 1.5 collective-permute-start.18
  97.2 2.7 %collective-permute-start.19 = (bf16[640,640]{1,0:T(8,128)(2,1)S(1)}, bf16[640,640]{1,0:T(8,128)(2,1)S(1)}, u32[]{:S(2)}, u32[]{:S(2)}) collective-permute-start(bf16[640,640]{1,0:T(8,128)(2,1)S(1)} %broadcast_select_fusion), channel_id=1, source_target_pairs={{0,4},{1,5},{2,6},{3,7},{4,8},{5,9},{6,10},{7,11},{8,12},{9,13},{1... | collective-permute-start | bytes 2457608 | tf_op jit(solution)/shard_map/ppermute | solution.py:36
  99.9 0.8 fusion.14
  100.7 1.8 %fusion.12 = f32[640,512]{1,0:T(8,128)S(1)} fusion(bf16[4,640,640]{2,1,0:T(8,128)(2,1)S(1)} %pad_maximum_fusion, s32[]{:T(128)S(6)} %select_n.201, bf16[640,512]{1,0:T(8,128)(2,1)S(1)} %collective-permute-done.10, bf16[640,512]{1,0:T(8,128)(2,1)S(1)} %collective-permute-done.9, bf16[640,512]{1,0:T(8,128)(2,1)} %collective-permute-done.7, ...), kind=kOutput, calls=%fused_computation.15 | convolution fusion | flops 420413440 | bytes 4751366 | tf_op jit(solution)/shard_map/dot_general | solution.py:107
  102.8 1.6 collective-permute-done.13
  104.3 5.3 %collective-permute-start.21 = (bf16[640,512]{1,0:T(8,128)(2,1)}, bf16[640,512]{1,0:T(8,128)(2,1)S(1)}, u32[]{:S(2)}, u32[]{:S(2)}) collective-permute-start(bf16[640,512]{1,0:T(8,128)(2,1)} %collective-permute-done.20), channel_id=1, source_target_pairs={{0,16},{2,18},{4,20},{6,22},{8,24},{10,26},{12,28},{14,30},{17,33}... | collective-permute-start | bytes 1966088 | tf_op jit(solution)/shard_map/ppermute | solution.py:36
  109.6 1.5 collective-permute-start.22
  111.2 0.7 fusion.10
  112.2 2.2 %collective-permute-done.17 = bf16[640,640]{1,0:T(8,128)(2,1)S(1)} collective-permute-done((bf16[640,640]{1,0:T(8,128)(2,1)S(1)}, bf16[640,640]{1,0:T(8,128)(2,1)S(1)}, u32[]{:S(2)}, u32[]{:S(2)}) %collective-permute-start.17) | collective-permute-done | bytes 819232 | tf_op jit(solution)/shard_map/ppermute | solution.py:36
  114.3 2.6 %collective-permute-start.23 = (bf16[640,512]{1,0:T(8,128)(2,1)}, bf16[640,512]{1,0:T(8,128)(2,1)S(1)}, u32[]{:S(2)}, u32[]{:S(2)}) collective-permute-start(bf16[640,512]{1,0:T(8,128)(2,1)} %collective-permute-done.20), channel_id=1, source_target_pairs={{0,32},{2,34},{4,36},{6,38},{8,40},{10,42},{12,44},{14,46},{17,49}... | collective-permute-start | bytes 1966088 | tf_op jit(solution)/shard_map/ppermute | solution.py:36
  116.9 13.3 %collective-permute-done.18 = bf16[640,640]{1,0:T(8,128)(2,1)S(1)} collective-permute-done((bf16[640,640]{1,0:T(8,128)(2,1)S(1)}, bf16[640,640]{1,0:T(8,128)(2,1)S(1)}, u32[]{:S(2)}, u32[]{:S(2)}) %collective-permute-start.18) | collective-permute-done | bytes 819232 | tf_op jit(solution)/shard_map/ppermute | solution.py:36
  130.3 0.5 pad_maximum_fusion.1
  130.8 0.7 fusion.8
  131.8 1.8 %fusion.6 = f32[640,512]{1,0:T(8,128)S(1)} fusion(bf16[4,640,640]{2,1,0:T(8,128)(2,1)S(1)} %pad_maximum_fusion.1, s32[]{:T(128)S(6)} %select_n.201, bf16[640,512]{1,0:T(8,128)(2,1)S(1)} %collective-permute-done.10, bf16[640,512]{1,0:T(8,128)(2,1)S(1)} %collective-permute-done.9, bf16[640,512]{1,0:T(8,128)(2,1)} %collective-permute-done.7, ...), kind=kOutput, calls=%fused_computation.9 | convolution fusion | flops 420413440 | bytes 4751366 | tf_op jit(solution)/shard_map/dot_general | solution.py:107
  133.9 0.7 fusion.4
  134.9 0.7 fusion.2
  135.9 0.7 fusion
  137.4 1.8 %collective-permute-done.24 = f32[640,256]{1,0:T(8,128)S(1)} collective-permute-done((f32[640,256]{1,0:T(8,128)S(1)}, f32[640,256]{1,0:T(8,128)S(1)}, u32[]{:S(2)}, u32[]{:S(2)}) %collective-permute-start.24) | collective-permute-done | bytes 655392 | tf_op jit(solution)/shard_map/ppermute | solution.py:36
  139.4 0.3 convolution_convert_fusion
  139.7 24.1 %all_to_all.5 = bf16[16,16,256]{2,1,0:T(8,128)(2,1)S(1)} all-to-all(bf16[16,16,256]{2,1,0:T(8,128)(2,1)S(1)} %bitcast.49), channel_id=1, replica_groups=mesh['zl'=4,'x'=4,'y'=4,'zh'=2,'core'=2] {'zl','x'}, dimensions={0} | all-to-all | bytes 262144 | tf_op jit(solution)/shard_map/all_to_all | solution.py:115
  163.8 0.6 bitcast_subtract_fusion
  (58 shorter events, 3.1 us)
Async XLA Ops:
  0.6 21.5 %collective-permute-start = (bf16[640,640]{1,0:T(8,128)(2,1)}, bf16[640,640]{1,0:T(8,128)(2,1)S(1)}, u32[]{:S(2)}, u32[]{:S(2)}) collective-permute-start(bf16[640,640]{1,0:T(8,128)(2,1)} %param.4), channel_id=1, source_target_pairs={{0,12},{1,13},{2,14},{3,15},{4,0},{5,1},{6,2},{7,3},{8,4},{9,5},{1... | collective-permute-start | bytes 2457608 | tf_op jit(solution)/shard_map/ppermute | solution.py:36
  3.6 90.3 %copy-start = (bf16[640,640]{1,0:T(8,128)(2,1)S(1)}, bf16[640,640]{1,0:T(8,128)(2,1)}, u32[]{:S(2)}) copy-start(bf16[640,640]{1,0:T(8,128)(2,1)} %param.4) | copy-start | bytes 2457604
  3.7 13.8 %collective-permute-start.3 = (bf16[640,256]{1,0:T(8,128)(2,1)S(1)}, bf16[640,256]{1,0:T(8,128)(2,1)S(1)}, u32[]{:S(2)}, u32[]{:S(2)}) collective-permute-start(bf16[640,256]{1,0:T(8,128)(2,1)S(1)} %broadcast_multiply_fusion), channel_id=1, source_target_pairs={{1,0},{3,2},{5,4},{7,6},{9,8},{11,10},{13,12},{15,14},{16,17},{18,... | collective-permute-start | bytes 983048 | tf_op jit(solution)/shard_map/ppermute | solution.py:36
  5.1 22.0 %collective-permute-start.2 = (bf16[640,640]{1,0:T(8,128)(2,1)}, bf16[640,640]{1,0:T(8,128)(2,1)S(1)}, u32[]{:S(2)}, u32[]{:S(2)}) collective-permute-start(bf16[640,640]{1,0:T(8,128)(2,1)} %param.4), channel_id=1, source_target_pairs={{0,4},{1,5},{2,6},{3,7},{4,8},{5,9},{6,10},{7,11},{8,12},{9,13},{1... | collective-permute-start | bytes 2457608 | tf_op jit(solution)/shard_map/ppermute | solution.py:36
  7.7 32.1 %collective-permute-start.15 = (bf16[640,640]{1,0:T(8,128)(2,1)}, bf16[640,640]{1,0:T(8,128)(2,1)S(1)}, u32[]{:S(2)}, u32[]{:S(2)}) collective-permute-start(bf16[640,640]{1,0:T(8,128)(2,1)} %param.4), channel_id=1, source_target_pairs={{0,2},{2,0},{4,6},{6,4},{8,10},{10,8},{12,14},{14,12},{17,19},{19,... | collective-permute-start | bytes 2457608 | tf_op jit(solution)/shard_map/ppermute | solution.py:36
  16.8 25.1 %collective-permute-start.16 = (bf16[640,640]{1,0:T(8,128)(2,1)}, bf16[640,640]{1,0:T(8,128)(2,1)S(1)}, u32[]{:S(2)}, u32[]{:S(2)}) collective-permute-start(bf16[640,640]{1,0:T(8,128)(2,1)} %param.4), channel_id=1, source_target_pairs={{1,3},{3,1},{5,7},{7,5},{9,11},{11,9},{13,15},{15,13},{16,18},{18,... | collective-permute-start | bytes 2457608 | tf_op jit(solution)/shard_map/ppermute | solution.py:36
  17.5 50.9 %copy-start.3 = (bf16[640,256]{1,0:T(8,128)(2,1)}, bf16[640,256]{1,0:T(8,128)(2,1)S(1)}, u32[]{:S(2)}) copy-start(bf16[640,256]{1,0:T(8,128)(2,1)S(1)} %collective-permute-done.3) | copy-start | bytes 983044
  17.5 40.3 %collective-permute-start.4 = (bf16[640,512]{1,0:T(8,128)(2,1)S(1)}, bf16[640,512]{1,0:T(8,128)(2,1)S(1)}, u32[]{:S(2)}, u32[]{:S(2)}) collective-permute-start(bf16[640,512]{1,0:T(8,128)(2,1)S(1)} %pad_maximum_fusion.2), channel_id=1, source_target_pairs={{0,16},{2,18},{4,20},{6,22},{8,24},{10,26},{12,28},{14,30},{17,33}... | collective-permute-start | bytes 1966088 | tf_op jit(solution)/shard_map/ppermute | solution.py:36
  22.1 46.2 %collective-permute-start.5 = (bf16[640,512]{1,0:T(8,128)(2,1)S(1)}, bf16[640,512]{1,0:T(8,128)(2,1)S(1)}, u32[]{:S(2)}, u32[]{:S(2)}) collective-permute-start(bf16[640,512]{1,0:T(8,128)(2,1)S(1)} %pad_maximum_fusion.2), channel_id=1, source_target_pairs={{0,32},{2,34},{4,36},{6,38},{8,40},{10,42},{12,44},{14,46},{17,49}... | collective-permute-start | bytes 1966088 | tf_op jit(solution)/shard_map/ppermute | solution.py:36
  27.1 42.2 %collective-permute-start.7 = (bf16[640,512]{1,0:T(8,128)(2,1)S(1)}, bf16[640,512]{1,0:T(8,128)(2,1)}, u32[]{:S(2)}, u32[]{:S(2)}) collective-permute-start(bf16[640,512]{1,0:T(8,128)(2,1)S(1)} %pad_maximum_fusion.2), channel_id=1, source_target_pairs={{0,192},{2,194},{4,196},{6,198},{8,200},{10,202},{12,204},{14,206}... | collective-permute-start | bytes 1966088 | tf_op jit(solution)/shard_map/ppermute | solution.py:36
  39.7 28.6 %copy-start.1 = (bf16[640,640]{1,0:T(8,128)(2,1)}, bf16[640,640]{1,0:T(8,128)(2,1)S(1)}, u32[]{:S(2)}) copy-start(bf16[640,640]{1,0:T(8,128)(2,1)S(1)} %collective-permute-done.15) | copy-start | bytes 2457604
  39.7 35.7 %collective-permute-start.6 = (bf16[640,512]{1,0:T(8,128)(2,1)S(1)}, bf16[640,512]{1,0:T(8,128)(2,1)}, u32[]{:S(2)}, u32[]{:S(2)}) collective-permute-start(bf16[640,512]{1,0:T(8,128)(2,1)S(1)} %pad_maximum_fusion.2), channel_id=1, source_target_pairs={{0,48},{2,50},{4,52},{6,54},{8,56},{10,58},{12,60},{14,62},{17,1},... | collective-permute-start | bytes 1966088 | tf_op jit(solution)/shard_map/ppermute | solution.py:36
  41.9 26.5 %copy-start.2 = (bf16[640,640]{1,0:T(8,128)(2,1)}, bf16[640,640]{1,0:T(8,128)(2,1)S(1)}, u32[]{:S(2)}) copy-start(bf16[640,640]{1,0:T(8,128)(2,1)S(1)} %collective-permute-done.16) | copy-start | bytes 2457604
  41.9 34.9 %collective-permute-start.11 = (bf16[640,512]{1,0:T(8,128)(2,1)S(1)}, bf16[640,512]{1,0:T(8,128)(2,1)}, u32[]{:S(2)}, u32[]{:S(2)}) collective-permute-start(bf16[640,512]{1,0:T(8,128)(2,1)S(1)} %pad_maximum_fusion.2), channel_id=1, source_target_pairs={{0,64},{2,66},{4,68},{6,70},{8,72},{10,74},{12,76},{14,78},{17,81}... | collective-permute-start | bytes 1966088 | tf_op jit(solution)/shard_map/ppermute | solution.py:36
  57.8 10.5 %copy-start.7 = (bf16[640,512]{1,0:T(8,128)(2,1)}, bf16[640,512]{1,0:T(8,128)(2,1)S(1)}, u32[]{:S(2)}) copy-start(bf16[640,512]{1,0:T(8,128)(2,1)S(1)} %collective-permute-done.4) | copy-start | bytes 1966084
  57.8 26.1 %collective-permute-start.20 = (bf16[640,512]{1,0:T(8,128)(2,1)S(1)}, bf16[640,512]{1,0:T(8,128)(2,1)}, u32[]{:S(2)}, u32[]{:S(2)}) collective-permute-start(bf16[640,512]{1,0:T(8,128)(2,1)S(1)} %pad_maximum_fusion.2), channel_id=1, source_target_pairs={{0,128},{2,130},{4,132},{6,134},{8,136},{10,138},{12,140},{14,142}... | collective-permute-start | bytes 1966088 | tf_op jit(solution)/shard_map/ppermute | solution.py:36
  68.4 0.8 copy-start.9
  69.2 18.4 %collective-permute-start.1 = (bf16[640,640]{1,0:T(8,128)(2,1)S(1)}, bf16[640,640]{1,0:T(8,128)(2,1)}, u32[]{:S(2)}, u32[]{:S(2)}) collective-permute-start(bf16[640,640]{1,0:T(8,128)(2,1)S(1)} %collective-permute-done), channel_id=1, source_target_pairs={{0,12},{1,13},{2,14},{3,15},{4,0},{5,1},{6,2},{7,3},{8,4},{9,5},{1... | collective-permute-start | bytes 2457608 | tf_op jit(solution)/shard_map/ppermute | solution.py:36
  69.2 19.7 %collective-permute-start.10 = (bf16[640,512]{1,0:T(8,128)(2,1)}, bf16[640,512]{1,0:T(8,128)(2,1)S(1)}, u32[]{:S(2)}, u32[]{:S(2)}) collective-permute-start(bf16[640,512]{1,0:T(8,128)(2,1)} %collective-permute-done.7), channel_id=1, source_target_pairs={{0,32},{2,34},{4,36},{6,38},{8,40},{10,42},{12,44},{14,46},{17,49}... | collective-permute-start | bytes 1966088 | tf_op jit(solution)/shard_map/ppermute | solution.py:36
  75.4 20.2 %collective-permute-start.8 = (bf16[640,512]{1,0:T(8,128)(2,1)}, bf16[640,512]{1,0:T(8,128)(2,1)S(1)}, u32[]{:S(2)}, u32[]{:S(2)}) collective-permute-start(bf16[640,512]{1,0:T(8,128)(2,1)} %collective-permute-done.7), channel_id=1, source_target_pairs={{0,16},{2,18},{4,20},{6,22},{8,24},{10,26},{12,28},{14,30},{17,33}... | collective-permute-start | bytes 1966088 | tf_op jit(solution)/shard_map/ppermute | solution.py:36
  76.8 19.0 %collective-permute-start.9 = (bf16[640,512]{1,0:T(8,128)(2,1)}, bf16[640,512]{1,0:T(8,128)(2,1)S(1)}, u32[]{:S(2)}, u32[]{:S(2)}) collective-permute-start(bf16[640,512]{1,0:T(8,128)(2,1)} %collective-permute-done.7), channel_id=1, source_target_pairs={{0,48},{2,50},{4,52},{6,54},{8,56},{10,58},{12,60},{14,62},{17,1},... | collective-permute-start | bytes 1966088 | tf_op jit(solution)/shard_map/ppermute | solution.py:36
  84.0 13.2 %collective-permute-start.12 = (bf16[640,512]{1,0:T(8,128)(2,1)}, bf16[640,512]{1,0:T(8,128)(2,1)S(1)}, u32[]{:S(2)}, u32[]{:S(2)}) collective-permute-start(bf16[640,512]{1,0:T(8,128)(2,1)} %collective-permute-done.11), channel_id=1, source_target_pairs={{0,16},{2,18},{4,20},{6,22},{8,24},{10,26},{12,28},{14,30},{17,33}... | collective-permute-start | bytes 1966088 | tf_op jit(solution)/shard_map/ppermute | solution.py:36
  87.6 16.7 %collective-permute-start.13 = (bf16[640,512]{1,0:T(8,128)(2,1)}, bf16[640,512]{1,0:T(8,128)(2,1)S(1)}, u32[]{:S(2)}, u32[]{:S(2)}) collective-permute-start(bf16[640,512]{1,0:T(8,128)(2,1)} %collective-permute-done.11), channel_id=1, source_target_pairs={{0,48},{2,50},{4,52},{6,54},{8,56},{10,58},{12,60},{14,62},{17,1},... | collective-permute-start | bytes 1966088 | tf_op jit(solution)/shard_map/ppermute | solution.py:36
  89.0 20.6 %collective-permute-start.14 = (bf16[640,512]{1,0:T(8,128)(2,1)}, bf16[640,512]{1,0:T(8,128)(2,1)S(1)}, u32[]{:S(2)}, u32[]{:S(2)}) collective-permute-start(bf16[640,512]{1,0:T(8,128)(2,1)} %collective-permute-done.11), channel_id=1, source_target_pairs={{0,32},{2,34},{4,36},{6,38},{8,40},{10,42},{12,44},{14,46},{17,49}... | collective-permute-start | bytes 1966088 | tf_op jit(solution)/shard_map/ppermute | solution.py:36
  93.9 5.9 %copy-start.4 = (bf16[640,256]{1,0:T(8,128)(2,1)S(1)}, bf16[640,256]{1,0:T(8,128)(2,1)}, u32[]{:S(2)}) copy-start(bf16[640,256]{1,0:T(8,128)(2,1)} %copy-done.3) | copy-start | bytes 983044
  93.9 5.9 %copy-start.8 = (bf16[640,512]{1,0:T(8,128)(2,1)S(1)}, bf16[640,512]{1,0:T(8,128)(2,1)}, u32[]{:S(2)}) copy-start(bf16[640,512]{1,0:T(8,128)(2,1)} %copy-done.7) | copy-start | bytes 1966084
  93.9 5.9 %copy-start.10 = (bf16[640,512]{1,0:T(8,128)(2,1)S(1)}, bf16[640,512]{1,0:T(8,128)(2,1)}, u32[]{:S(2)}) copy-start(bf16[640,512]{1,0:T(8,128)(2,1)} %copy-done.9) | copy-start | bytes 1966084
  95.6 18.7 %collective-permute-start.17 = (bf16[640,640]{1,0:T(8,128)(2,1)S(1)}, bf16[640,640]{1,0:T(8,128)(2,1)S(1)}, u32[]{:S(2)}, u32[]{:S(2)}) collective-permute-start(bf16[640,640]{1,0:T(8,128)(2,1)S(1)} %broadcast_select_fusion), channel_id=1, source_target_pairs={{0,12},{1,13},{2,14},{3,15},{4,0},{5,1},{6,2},{7,3},{8,4},{9,5},{1... | collective-permute-start | bytes 2457608 | tf_op jit(solution)/shard_map/ppermute | solution.py:36
  95.7 34.5 %collective-permute-start.18 = (bf16[640,640]{1,0:T(8,128)(2,1)S(1)}, bf16[640,640]{1,0:T(8,128)(2,1)S(1)}, u32[]{:S(2)}, u32[]{:S(2)}) collective-permute-start(bf16[640,640]{1,0:T(8,128)(2,1)S(1)} %broadcast_select_fusion), channel_id=1, source_target_pairs={{0,8},{1,9},{2,10},{3,11},{4,12},{5,13},{6,14},{7,15},{8,0},{9,1},... | collective-permute-start | bytes 2457608 | tf_op jit(solution)/shard_map/ppermute | solution.py:36
  97.2 33.1 %collective-permute-start.19 = (bf16[640,640]{1,0:T(8,128)(2,1)S(1)}, bf16[640,640]{1,0:T(8,128)(2,1)S(1)}, u32[]{:S(2)}, u32[]{:S(2)}) collective-permute-start(bf16[640,640]{1,0:T(8,128)(2,1)S(1)} %broadcast_select_fusion), channel_id=1, source_target_pairs={{0,4},{1,5},{2,6},{3,7},{4,8},{5,9},{6,10},{7,11},{8,12},{9,13},{1... | collective-permute-start | bytes 2457608 | tf_op jit(solution)/shard_map/ppermute | solution.py:36
  104.3 30.6 %collective-permute-start.21 = (bf16[640,512]{1,0:T(8,128)(2,1)}, bf16[640,512]{1,0:T(8,128)(2,1)S(1)}, u32[]{:S(2)}, u32[]{:S(2)}) collective-permute-start(bf16[640,512]{1,0:T(8,128)(2,1)} %collective-permute-done.20), channel_id=1, source_target_pairs={{0,16},{2,18},{4,20},{6,22},{8,24},{10,26},{12,28},{14,30},{17,33}... | collective-permute-start | bytes 1966088 | tf_op jit(solution)/shard_map/ppermute | solution.py:36
  109.6 25.3 %collective-permute-start.22 = (bf16[640,512]{1,0:T(8,128)(2,1)}, bf16[640,512]{1,0:T(8,128)(2,1)S(1)}, u32[]{:S(2)}, u32[]{:S(2)}) collective-permute-start(bf16[640,512]{1,0:T(8,128)(2,1)} %collective-permute-done.20), channel_id=1, source_target_pairs={{0,48},{2,50},{4,52},{6,54},{8,56},{10,58},{12,60},{14,62},{17,1},... | collective-permute-start | bytes 1966088 | tf_op jit(solution)/shard_map/ppermute | solution.py:36
  114.3 20.6 %collective-permute-start.23 = (bf16[640,512]{1,0:T(8,128)(2,1)}, bf16[640,512]{1,0:T(8,128)(2,1)S(1)}, u32[]{:S(2)}, u32[]{:S(2)}) collective-permute-start(bf16[640,512]{1,0:T(8,128)(2,1)} %collective-permute-done.20), channel_id=1, source_target_pairs={{0,32},{2,34},{4,36},{6,38},{8,40},{10,42},{12,44},{14,46},{17,49}... | collective-permute-start | bytes 1966088 | tf_op jit(solution)/shard_map/ppermute | solution.py:36
  136.6 27.1 %copy-start.6 = (f32[1,16,256]{2,1,0:T(8,128)S(1)}, f32[1,16,256]{2,1,0:T(8,128)}, u32[]{:S(2)}) copy-start(f32[1,16,256]{2,1,0:T(8,128)} %param.6) | copy-start | bytes 49156
  137.0 2.2 %collective-permute-start.24 = (f32[640,256]{1,0:T(8,128)S(1)}, f32[640,256]{1,0:T(8,128)S(1)}, u32[]{:S(2)}, u32[]{:S(2)}) collective-permute-start(f32[640,256]{1,0:T(8,128)S(1)} %slice.9), channel_id=1, source_target_pairs={{0,1},{1,0},{2,3},{3,2},{4,5},{5,4},{6,7},{7,6},{8,9},{9,8},{10,11... | collective-permute-start | bytes 1966088 | tf_op jit(solution)/shard_map/ppermute | solution.py:36
  139.4 25.0 %copy-start.5 = (bf16[640,256]{1,0:T(8,128)(2,1)}, bf16[640,256]{1,0:T(8,128)(2,1)S(1)}, u32[]{:S(2)}) copy-start(bf16[640,256]{1,0:T(8,128)(2,1)S(1)} %fusion.26) | copy-start | bytes 983044
